TPU v7x, 128 devices: a whole 4x4x4 slice. The times are simulated.
128 devices in a mesh: ha: 16 (over z, y_lo, core), wa: 8 (over x, y_hi).
Axes of the slice: x: 4, y: 4 (y_hi: 2, y_lo: 2; y = y_hi * 2 + y_lo), z: 4, core: 2. Of those that a mesh axis runs over, the one named last changes fastest.
Arguments:
- tokens: bfloat16 [256, 256, 512], P('ha', 'wa'), may hold values from -40 to 40
- cotangent: bfloat16 [256, 256, 512], P('ha', 'wa'), may hold values from -6 to 6
- norm_gain: float32 [512], replicated, may hold values from 0.1 to 1.9
- in_weight: bfloat16 [512, 1536], replicated, may hold values from -0.25 to 0.25
- out_weight: bfloat16 [512, 512], replicated, may hold values from -0.25 to 0.25
- bias_table: float32 [16, 31, 31], replicated, may hold values from -256 to 256
Outputs:
- grad_input: bfloat16 [256, 256, 512], P('ha', 'wa')
- grad_table: float32 [16, 31, 31], replicated
All inputs are finite; a program needn't handle non-finite values.
Results may differ from a plain program's by a relative error of at most 0.011.
Values may be sent and summed in bfloat16 or wider, within the bound.
No kernel may reach another device: no remote copies, remote signals or barrier semaphores. Data moves between devices by JAX's collectives and lax.ppermute only.
A program may use at most 128 MiB of HBM per device.

v0:
```python
import jax
import jax.numpy as jnp
from jax import lax
from jax.sharding import PartitionSpec as P

D = 512
HEADS = 16
HEAD_DIM = 32
WIN = 16
TAB = 31


NORM_EPS = 1e-05


def offset_hot():
    places = jnp.arange(WIN)
    slot_ids = jnp.arange(TAB)
    return (
        places[:, None, None] - places[None, :, None] + (WIN - 1) == slot_ids[None, None, :]
    ).astype(jnp.float32)


def full_bias(bias_table, offset_table):
    partial_rows = jnp.einsum(
        "abd,hde->habe", offset_table, bias_table, precision=lax.Precision.HIGHEST
    )
    spread = jnp.einsum(
        "uve,habe->haubv", offset_table, partial_rows, precision=lax.Precision.HIGHEST
    )
    return spread.reshape(HEADS, WIN * WIN, WIN * WIN)


def group_grad(group_tokens, group_cot, norm_gain, in_weight, out_weight, bias_full, offset_table):
    group_rows = WIN * WIN
    tokens_wide = group_tokens.astype(jnp.float32)
    center = jnp.mean(tokens_wide, axis=-1, keepdims=True)
    shifted = tokens_wide - center
    inv_std = lax.rsqrt(jnp.mean(shifted * shifted, axis=-1, keepdims=True) + NORM_EPS)
    unit_rows = shifted * inv_std
    normed = (unit_rows * norm_gain).astype(jnp.bfloat16)
    mixed_rows = jnp.dot(normed, in_weight, preferred_element_type=jnp.float32)
    query_scale = HEAD_DIM ** (-0.5)
    queries = (
        (mixed_rows[:, :D] * query_scale).astype(jnp.bfloat16).reshape(group_rows, HEADS, HEAD_DIM)
    )
    key_rows = mixed_rows[:, D : 2 * D].astype(jnp.bfloat16).reshape(group_rows, HEADS, HEAD_DIM)
    values = mixed_rows[:, 2 * D :].astype(jnp.bfloat16).reshape(group_rows, HEADS, HEAD_DIM)
    scores = (
        jnp.einsum("thd,shd->hts", queries, key_rows, preferred_element_type=jnp.float32)
        + bias_full
    )
    row_top = jnp.max(scores, axis=-1, keepdims=True)
    exponent = jnp.exp(scores - row_top)
    attn_probs = exponent / jnp.sum(exponent, axis=-1, keepdims=True)
    probs_half = attn_probs.astype(jnp.bfloat16)
    grad_out = lax.dot_general(
        group_cot, out_weight, (((1,), (1,)), ((), ())), preferred_element_type=jnp.float32
    )
    grad_out = grad_out.astype(jnp.bfloat16).reshape(group_rows, HEADS, HEAD_DIM)
    grad_probs = jnp.einsum("thd,shd->hts", grad_out, values, preferred_element_type=jnp.float32)
    grad_values = jnp.einsum(
        "hts,thd->shd", probs_half, grad_out, preferred_element_type=jnp.float32
    ).astype(jnp.bfloat16)
    grad_scores = attn_probs * (
        grad_probs - jnp.sum(attn_probs * grad_probs, axis=-1, keepdims=True)
    )
    scores_half = grad_scores.astype(jnp.bfloat16)
    grad_queries = (
        jnp.einsum("hts,shd->thd", scores_half, key_rows, preferred_element_type=jnp.float32)
        * query_scale
    ).astype(jnp.bfloat16)
    grad_keys = jnp.einsum(
        "hts,thd->shd", scores_half, queries, preferred_element_type=jnp.float32
    ).astype(jnp.bfloat16)
    grad_mixed = jnp.concatenate(
        [
            grad_queries.reshape(group_rows, D),
            grad_keys.reshape(group_rows, D),
            grad_values.reshape(group_rows, D),
        ],
        axis=1,
    )
    grad_normed = lax.dot_general(
        grad_mixed, in_weight, (((1,), (1,)), ((), ())), preferred_element_type=jnp.float32
    )
    grad_unit = grad_normed * norm_gain
    grad_rows = inv_std * (
        grad_unit
        - jnp.mean(grad_unit, axis=-1, keepdims=True)
        - unit_rows * jnp.mean(grad_unit * unit_rows, axis=-1, keepdims=True)
    )
    folded = jnp.einsum(
        "haubv,uve->habe",
        grad_scores.reshape(HEADS, WIN, WIN, WIN, WIN),
        offset_table,
        precision=lax.Precision.HIGHEST,
    )
    table_part = jnp.einsum("habe,abd->hde", folded, offset_table, precision=lax.Precision.HIGHEST)
    return (grad_rows.astype(jnp.bfloat16), table_part)


def body(tokens, cotangent, norm_gain, in_weight, out_weight, bias_table):
    offset_table = offset_hot()
    bias_full = full_bias(bias_table, offset_table)
    high_parts = lax.axis_size("ha")
    wide_parts = lax.axis_size("wa")
    rows_local, cols_local, channels = tokens.shape
    row_steps = WIN // high_parts
    col_steps = WIN // wide_parts
    stride_h = rows_local // row_steps
    stride_w = cols_local // col_steps
    row_groups = stride_h // high_parts
    col_groups = stride_w // wide_parts
    group_count = row_groups * col_groups

    def to_layout(tile_block):
        laid = tile_block.reshape(
            row_steps, high_parts, row_groups, col_steps, wide_parts, col_groups, channels
        )
        laid = laid.transpose(2, 5, 1, 4, 0, 3, 6)
        return laid.reshape(group_count, high_parts, wide_parts, row_steps, col_steps, channels)

    def one_group(pair_rows):
        return group_grad(
            pair_rows[0], pair_rows[1], norm_gain, in_weight, out_weight, bias_full, offset_table
        )

    laid_tokens = to_layout(tokens)
    laid_cot = to_layout(cotangent)

    def swap_rows(laid):
        items = laid.shape[0]
        shaped = laid.reshape(items, high_parts, wide_parts, row_steps, col_steps, channels)
        return shaped.transpose(0, 1, 3, 2, 4, 5).reshape(items, WIN * WIN, channels)

    flat_shape = (group_count, high_parts * wide_parts, row_steps * col_steps, channels)
    grad_rows, table_parts = lax.map(
        one_group,
        (
            swap_rows(
                lax.all_to_all(
                    laid_tokens.reshape(flat_shape),
                    ("ha", "wa"),
                    split_axis=1,
                    concat_axis=1,
                    tiled=True,
                )
            ),
            swap_rows(
                lax.all_to_all(
                    laid_cot.reshape(flat_shape),
                    ("ha", "wa"),
                    split_axis=1,
                    concat_axis=1,
                    tiled=True,
                )
            ),
        ),
    )
    items = grad_rows.shape[0]
    shaped = grad_rows.reshape(items, high_parts, row_steps, wide_parts, col_steps, channels)
    grads_laid, table_parts = (
        shaped.transpose(0, 1, 3, 2, 4, 5).reshape(
            items, high_parts * wide_parts, row_steps * col_steps, channels
        ),
        table_parts,
    )
    returned = lax.all_to_all(grads_laid, ("ha", "wa"), split_axis=1, concat_axis=1, tiled=True)
    returned = returned.reshape(group_count, high_parts, wide_parts, row_steps, col_steps, channels)
    shaped = returned.reshape(
        row_groups, col_groups, high_parts, wide_parts, row_steps, col_steps, channels
    )
    shaped = shaped.transpose(4, 2, 0, 5, 3, 1, 6)
    grad_input = shaped.reshape(rows_local, cols_local, channels)
    grad_table = lax.psum(jnp.sum(table_parts, axis=0), ("ha", "wa"))
    return (grad_input, grad_table)


def solution(mesh):
    in_specs = (P("ha", "wa", None), P("ha", "wa", None), P(), P(), P(), P())
    out_specs = (P("ha", "wa", None), P())
    return jax.shard_map(body, mesh=mesh, in_specs=in_specs, out_specs=out_specs, check_vma=False)
```

profile of v0, /device:TPU:1, one launch (start us, length us, event | category | flops | bytes accessed | tf_op | source)
XLA Modules:
  0.0 330.3 jit_solution(11427729656623690947)
XLA Ops:
  0.6 1.3 reshape.82
  1.9 1.6 copy.72
  3.5 11.5 %all-to-all-start = ((bf16[2,128,2,512]{3,2,0,1:T(2,128)(2,1)}), bf16[2,128,2,512]{3,2,0,1:T(2,128)(2,1)S(1)}, u32[]{:S(2)}, u32[]{:S(2)}) async-start(bf16[2,128,2,512]{3,2,0,1:T(2,128)(2,1)} %bitcast.1), calls=%async_computation | async-start | bytes 1048576 | tf_op jit(solution)/shard_map/all_to_all | solution.py:142
  15.7 1.2 reshape.84
  17.0 1.6 copy.76
  18.6 1.0 fusion.54
  19.6 9.5 %all-to-all-done = bf16[2,128,2,512]{3,2,0,1:T(2,128)(2,1)S(1)} async-done(((bf16[2,128,2,512]{3,2,0,1:T(2,128)(2,1)}), bf16[2,128,2,512]{3,2,0,1:T(2,128)(2,1)S(1)}, u32[]{:S(2)}, u32[]{:S(2)}) %all-to-all-start) | async-done | bytes 524320 | tf_op jit(solution)/shard_map/all_to_all | solution.py:142
  29.1 4.7 %all-to-all-start.1 = ((bf16[2,128,2,512]{3,2,0,1:T(2,128)(2,1)}), bf16[2,128,2,512]{3,2,0,1:T(2,128)(2,1)}, u32[]{:S(2)}, u32[]{:S(2)}) async-start(bf16[2,128,2,512]{3,2,0,1:T(2,128)(2,1)} %bitcast.12), calls=%async_computation.1 | async-start | bytes 1048576 | tf_op jit(solution)/shard_map/all_to_all | solution.py:151
  33.8 17.4 %convolution_bitcast_fusion = f32[16,16,16,16,16]{4,3,2,1,0:T(8,128)} fusion(f32[16,16,16,31]{3,1,0,2:T(8,128)S(1)} %fusion.54, s32[16,16]{1,0:T(8,128)S(1)} %copy.74), kind=kOutput, calls=%fused_computation.64 | convolution fusion | flops 390078208 | bytes 4703232 | tf_op jit(solution)/shard_map/uve,habe->haubv/dot_general | solution.py:28
  51.2 23.5 %reshape.83 = f32[16,256,256]{2,1,0:T(8,128)} reshape(f32[16,16,16,16,16]{4,3,2,1,0:T(8,128)} %convolution_bitcast_fusion) | data formatting | bytes 8388608 | tf_op jit(solution)/shard_map/reshape | solution.py:31
  74.7 5.4 %copy.79 = f32[16,256,256]{1,2,0:T(8,128)} copy(f32[16,256,256]{2,1,0:T(8,128)} %reshape.83) | data formatting | bytes 8388608
  80.7 1.6 copy.77
  82.3 0.9 copy.80
  83.1 162.9 %while.14 = (s32[]{:T(128)}, bf16[2,256,512]{2,1,0:T(8,128)(2,1)}, f32[2,16,31,31]{2,3,1,0:T(8,128)}, bf16[2,256,512]{2,1,0:T(8,128)(2,1)S(1)}, f32[512]{0:T(512...) while((s32[]{:T(128)}, bf16[2,256,512]{2,1,0:T(8,128)(2,1)}, ...), condition=%wide.region_8.9_spmd.clone.clone, body=%wide.region_0.8_spmd.clone.clone.sunk | while | flops 1734164224 | bytes 137940368 | solution.py:138
  83.7 1.3 convolution_convert_fusion.4
  85.0 0.9 copy.105
  87.2 1.1 copy.106
  88.3 0.8 fusion.129
  89.2 1.1 copy.107
  90.3 1.1 copy.108
  91.3 2.9 convolution_add_fusion.2
  94.3 3.1 fusion.130
  97.5 5.2 %fusion.131 = bf16[16,32,256]{2,1,0:T(8,128)(2,1)} fusion(bf16[256,16,32]{0,2,1:T(8,128)(2,1)S(1)} %bitcast.193, f32[16,256]{1,0:T(8,128)S(1)} %get-tuple-element.273, f32[16,256,256]{1,2,0:T(8,128)} %copy-done.4), kind=kOutput, calls=%fused_computation.13.clone.1 | convolution fusion | flops 70390016 | bytes 4734976 | tf_op jit(solution)/shard_map/while/body/eval_jaxpr/hts,thd->shd/dot_general | solution.py:62
  102.7 3.2 multiply_reduce_fusion.2
  109.6 0.9 fusion.134
  110.5 19.4 %reshape.111 = f32[16,16,16,16,16]{2,1,4,3,0:T(8,128)} reshape(f32[16,256,256]{1,2,0:T(8,128)} %copy-done.2) | data formatting | bytes 8388608 | tf_op jit(solution)/shard_map/while/body/eval_jaxpr/reshape | solution.py:95
  129.9 30.4 %fusion.135 = f32[16,16,16,31,1]{3,1,4,2,0:T(8,128)S(1)} fusion(f32[16,16,16,16,16]{2,1,4,3,0:T(8,128)} %reshape.111, s32[16,16]{0,1:T(8,128)S(1)} %get-tuple-element.314), kind=kOutput, calls=%fused_computation.53.clone.1 | convolution fusion | flops 390086144 | bytes 4703232 | tf_op jit(solution)/shard_map/while/body/eval_jaxpr/haubv,uve->habe/dot_general | solution.py:93
  160.4 3.5 %fusion.136 = f32[2,16,31,31]{2,3,1,0:T(8,128)S(1)} fusion(f32[2,16,31,31]{2,3,1,0:T(8,128)S(1)} %copy-done.13, s32[]{:T(128)S(6)} %copy.114, f32[16,16,16,31,1]{3,1,4,2,0:T(8,128)S(1)} %fusion.135, s32[16,16]{0,1:T(8,128)S(1)} %get-tuple-element.314), kind=kOutput, calls=%fused_computation.18.clone.1 | convolution fusion | flops 47250944 | bytes 2367492 | tf_op jit(solution)/shard_map/while/body/eval_jaxpr/habe,abd->hde/dot_general | solution.py:99
  165.0 1.3 convolution_convert_fusion.4
  166.3 0.9 copy.105
  168.6 1.1 copy.106
  169.7 0.8 fusion.129
  170.5 1.1 copy.107
  171.6 1.1 copy.108
  172.7 2.9 convolution_add_fusion.2
  175.6 3.1 fusion.130
  178.8 5.2 %fusion.131 = bf16[16,32,256]{2,1,0:T(8,128)(2,1)} fusion(bf16[256,16,32]{0,2,1:T(8,128)(2,1)S(1)} %bitcast.193, f32[16,256]{1,0:T(8,128)S(1)} %get-tuple-element.273, f32[16,256,256]{1,2,0:T(8,128)} %copy-done.4), kind=kOutput, calls=%fused_computation.13.clone.1 | convolution fusion | flops 70390016 | bytes 4734976 | tf_op jit(solution)/shard_map/while/body/eval_jaxpr/hts,thd->shd/dot_general | solution.py:62
  184.0 3.2 multiply_reduce_fusion.2
  190.9 0.9 fusion.134
  191.9 19.4 %reshape.111 = f32[16,16,16,16,16]{2,1,4,3,0:T(8,128)} reshape(f32[16,256,256]{1,2,0:T(8,128)} %copy-done.2) | data formatting | bytes 8388608 | tf_op jit(solution)/shard_map/while/body/eval_jaxpr/reshape | solution.py:95
  211.3 30.4 %fusion.135 = f32[16,16,16,31,1]{3,1,4,2,0:T(8,128)S(1)} fusion(f32[16,16,16,16,16]{2,1,4,3,0:T(8,128)} %reshape.111, s32[16,16]{0,1:T(8,128)S(1)} %get-tuple-element.314), kind=kOutput, calls=%fused_computation.53.clone.1 | convolution fusion | flops 390086144 | bytes 4703232 | tf_op jit(solution)/shard_map/while/body/eval_jaxpr/haubv,uve->habe/dot_general | solution.py:93
  241.7 3.5 %fusion.136 = f32[2,16,31,31]{2,3,1,0:T(8,128)S(1)} fusion(f32[2,16,31,31]{2,3,1,0:T(8,128)S(1)} %copy-done.13, s32[]{:T(128)S(6)} %copy.114, f32[16,16,16,31,1]{3,1,4,2,0:T(8,128)S(1)} %fusion.135, s32[16,16]{0,1:T(8,128)S(1)} %get-tuple-element.314), kind=kOutput, calls=%fused_computation.18.clone.1 | convolution fusion | flops 47250944 | bytes 2367492 | tf_op jit(solution)/shard_map/while/body/eval_jaxpr/habe,abd->hde/dot_general | solution.py:99
  246.0 2.4 copy.81
  248.4 9.9 %all-to-all-start.2 = ((bf16[2,128,2,512]{3,0,2,1:T(2,128)(2,1)}), bf16[2,128,2,512]{3,0,2,1:T(2,128)(2,1)S(1)}, u32[]{:S(2)}, u32[]{:S(2)}) async-start(bf16[2,128,2,512]{3,0,2,1:T(2,128)(2,1)} %bitcast.14), calls=%async_computation.2 | async-start | bytes 1048576 | tf_op jit(solution)/shard_map/all_to_all | solution.py:169
  258.3 1.1 reduce_sum.63
  259.4 68.6 %psum.7 = f32[16,31,31]{1,2,0:T(8,128)S(1)} all-reduce(f32[16,31,31]{1,2,0:T(8,128)S(1)} %reduce_sum.63), channel_id=1, replica_groups=mesh['ha'=16,'wa'=8] {'ha','wa'}, use_global_device_ids=true, to_apply=%region_10.11 | all-reduce | flops 15376 | bytes 123008 | tf_op jit(solution)/shard_map/psum | solution.py:176
  328.0 0.9 copy.85
  329.2 1.1 copy.84
  (82 shorter events, 14.2 us)
Async XLA Ops:
  0.6 18.0 %copy-start = (f32[16,31,31]{2,0,1:T(8,128)S(1)}, f32[16,31,31]{2,0,1:T(8,128)}, u32[]{:S(2)}) copy-start(f32[16,31,31]{2,0,1:T(8,128)} %param.13) | copy-start | bytes 184516
  3.5 25.5 %all-to-all-start = ((bf16[2,128,2,512]{3,2,0,1:T(2,128)(2,1)}), bf16[2,128,2,512]{3,2,0,1:T(2,128)(2,1)S(1)}, u32[]{:S(2)}, u32[]{:S(2)}) async-start(bf16[2,128,2,512]{3,2,0,1:T(2,128)(2,1)} %bitcast.1), calls=%async_computation | async-start | bytes 1048576 | tf_op jit(solution)/shard_map/all_to_all | solution.py:142
  15.0 0.6 copy-start.11
  29.1 22.1 %copy-start.9 = (bf16[2,128,2,512]{3,2,0,1:T(2,128)(2,1)}, bf16[2,128,2,512]{3,2,0,1:T(2,128)(2,1)S(1)}, u32[]{:S(2)}) copy-start(bf16[2,128,2,512]{3,2,0,1:T(2,128)(2,1)S(1)} %all-to-all-done) | copy-start | bytes 1572868
  29.1 51.6 %all-to-all-start.1 = ((bf16[2,128,2,512]{3,2,0,1:T(2,128)(2,1)}), bf16[2,128,2,512]{3,2,0,1:T(2,128)(2,1)}, u32[]{:S(2)}, u32[]{:S(2)}) async-start(bf16[2,128,2,512]{3,2,0,1:T(2,128)(2,1)} %bitcast.12), calls=%async_computation.1 | async-start | bytes 1048576 | tf_op jit(solution)/shard_map/all_to_all | solution.py:151
  74.7 5.4 %copy-start.10 = (bf16[2,128,2,512]{3,2,0,1:T(2,128)(2,1)S(1)}, bf16[2,128,2,512]{3,2,0,1:T(2,128)(2,1)}, u32[]{:S(2)}) copy-start(bf16[2,128,2,512]{3,2,0,1:T(2,128)(2,1)} %copy-done.9) | copy-start | bytes 1572868
  80.1 3.0 copy-start.5
  80.1 3.0 copy-start.6
  80.2 3.0 copy-start.12
  80.2 3.0 copy-start.15
  94.3 3.2 copy-start.4
  94.3 3.2 copy-start.8
  102.7 3.4 %copy-start.3 = (f32[16,256,256]{1,2,0:T(8,128)S(1)}, f32[16,256,256]{1,2,0:T(8,128)}, u32[]{:S(2)}) copy-start(f32[16,256,256]{1,2,0:T(8,128)} %get-tuple-element.274) | copy-start | bytes 12582916 | tf_op jit(solution)/shard_map/while
  106.9 2.0 copy-start.2
  106.9 2.0 copy-start.16
  129.9 30.4 %copy-start.13 = (f32[2,16,31,31]{2,3,1,0:T(8,128)S(1)}, f32[2,16,31,31]{2,3,1,0:T(8,128)}, u32[]{:S(2)}) copy-start(f32[2,16,31,31]{2,3,1,0:T(8,128)} %get-tuple-element.296) | copy-start | bytes 369028 | tf_op jit(solution)/shard_map/while
  129.9 34.7 %copy-start.7 = (bf16[512,512]{1,0:T(8,128)(2,1)S(1)}, bf16[512,512]{1,0:T(8,128)(2,1)}, u32[]{:S(2)}) copy-start(bf16[512,512]{1,0:T(8,128)(2,1)} %get-tuple-element.327) | copy-start | bytes 1572868 | tf_op jit(solution)/shard_map/while
  163.9 0.8 copy-start.14
  175.6 3.2 copy-start.4
  175.6 3.2 copy-start.8
  184.0 3.4 %copy-start.3 = (f32[16,256,256]{1,2,0:T(8,128)S(1)}, f32[16,256,256]{1,2,0:T(8,128)}, u32[]{:S(2)}) copy-start(f32[16,256,256]{1,2,0:T(8,128)} %get-tuple-element.274) | copy-start | bytes 12582916 | tf_op jit(solution)/shard_map/while
  188.2 2.0 copy-start.2
  188.2 2.0 copy-start.16
  211.3 30.4 %copy-start.13 = (f32[2,16,31,31]{2,3,1,0:T(8,128)S(1)}, f32[2,16,31,31]{2,3,1,0:T(8,128)}, u32[]{:S(2)}) copy-start(f32[2,16,31,31]{2,3,1,0:T(8,128)} %get-tuple-element.296) | copy-start | bytes 369028 | tf_op jit(solution)/shard_map/while
  211.3 34.7 %copy-start.7 = (bf16[512,512]{1,0:T(8,128)(2,1)S(1)}, bf16[512,512]{1,0:T(8,128)(2,1)}, u32[]{:S(2)}) copy-start(bf16[512,512]{1,0:T(8,128)(2,1)} %get-tuple-element.327) | copy-start | bytes 1572868 | tf_op jit(solution)/shard_map/while
  245.2 0.8 copy-start.14
  246.0 84.3 %copy-start.1 = (f32[16,31,31]{2,0,1:T(8,128)S(1)}, f32[16,31,31]{2,0,1:T(8,128)}, u32[]{:S(2)}) copy-start(f32[16,31,31]{2,0,1:T(8,128)} %param.13) | copy-start | bytes 184516
  248.4 80.5 %all-to-all-start.2 = ((bf16[2,128,2,512]{3,0,2,1:T(2,128)(2,1)}), bf16[2,128,2,512]{3,0,2,1:T(2,128)(2,1)S(1)}, u32[]{:S(2)}, u32[]{:S(2)}) async-start(bf16[2,128,2,512]{3,0,2,1:T(2,128)(2,1)} %bitcast.14), calls=%async_computation.2 | async-start | bytes 1048576 | tf_op jit(solution)/shard_map/all_to_all | solution.py:169
where the time goes:
time: 332 us; the launch traced here: 330 us
  matrix products  117 us (35%)
  local copies, waits for them, and re-layouts  95.5 us (29%)
  blocking collectives  68.6 us (21%)
  starting transfers between devices  26.1 us (8%)
  other arithmetic  12.9 us (4%)
  waiting for transfers between devices  9.46 us (3%)
    psum x1, blocking collectives, body(): grad_table = lax.psum(jnp.sum(table_parts, axis=0), ('ha', 'wa'))  68.6 us
    dot_general x2, matrix products, group_grad(): jnp.einsum('haubv,uve->habe', grad_scores.reshape(HEADS, WIN, WIN, WIN, W...  60.8 us
    reshape x2, local copies, waits for them, and re-layouts, group_grad(): grad_scores.reshape(HEADS, WIN, WIN, WIN, WIN)  38.8 us
    reshape x1, local copies, waits for them, and re-layouts, full_bias(): return spread.reshape(HEADS, WIN * WIN, WIN * WIN)  23.5 us
    dot_general x1, matrix products, full_bias(): jnp.einsum('uve,habe->haubv', offset_table, partial_rows, precision=lax.P...  17.4 us
    all_to_all x1, starting transfers between devices, body(): lax.all_to_all(laid_tokens.reshape(flat_shape), ('ha', 'wa'), split_axis=...  11.5 us
    dot_general x2, matrix products, group_grad(): jnp.einsum('hts,thd->shd', probs_half, grad_out, preferred_element_type=j...  10.3 us
    all_to_all x1, starting transfers between devices, body(): lax.all_to_all(grads_laid, ('ha', 'wa'), split_axis=1, concat_axis=1, til...  9.89 us
  transfers between devices with their start and end apart: 3, of which 1 were waited for; matrix products, arithmetic and copies ran while one was open for 16% of the time, Pallas kernels for 0%

commit v1 on v0

v1 whole, which is shorter than its diff:
```python
import jax
import jax.numpy as jnp
from jax import lax
from jax.experimental import pallas as pl
from jax.experimental.pallas import tpu as pltpu
from jax.sharding import PartitionSpec as P

D = 512
HEADS = 16
HEAD_DIM = 32
WIN = 16
TAB = 31
NORM_EPS = 1e-05
AXES = ("ha", "wa")
BF16 = jnp.bfloat16
F32 = jnp.float32


def iota(shape, dim):
    return lax.broadcasted_iota(jnp.int32, shape, dim)


def bits(x, low, count):
    return lax.bitwise_and(lax.shift_right_logical(x, low), (1 << count) - 1)


def one_hot(source):
    o = iota((256, 256), 0)
    return jnp.where(source(o) == iota((256, 256), 1), 1.0, 0.0).astype(BF16)


def move_rows(matrix, rows):
    return jnp.dot(matrix, rows, preferred_element_type=F32).astype(BF16)


def pack_kernel(tok_ref, cot_ref, out_ref):
    perm = one_hot(
        lambda o: bits(o, 2, 1) * 128
        + bits(o, 6, 2) * 32
        + bits(o, 0, 1) * 16
        + bits(o, 3, 3) * 2
        + bits(o, 1, 1)
    )
    for q in range(4):
        rows = jnp.concatenate(
            [
                tok_ref[4 * q : 4 * q + 4].reshape(128, D),
                cot_ref[4 * q : 4 * q + 4].reshape(128, D),
            ],
            axis=0,
        )
        out_ref[256 * q : 256 * q + 256, :] = move_rows(perm, rows)


def unpack_kernel(in_ref, out_ref):
    perm = one_hot(
        lambda o: bits(o, 5, 2) * 64
        + bits(o, 1, 3) * 8
        + bits(o, 7, 1) * 4
        + bits(o, 0, 1) * 2
        + bits(o, 4, 1)
    )
    for q in range(4):
        rows = move_rows(perm, in_ref[256 * q : 256 * q + 256, :])
        out_ref[4 * q : 4 * q + 4, :, 0:256] = rows[0:128].reshape(4, 32, 256)
        out_ref[4 * q : 4 * q + 4, :, 256:512] = rows[128:256].reshape(4, 32, 256)


def dot_nt(a, b):
    return lax.dot_general(a, b, (((1,), (1,)), ((), ())), preferred_element_type=F32)


def dot_nn(a, b):
    return jnp.dot(a, b, preferred_element_type=F32)


def group_kernel(
    recv_ref, gain_ref, win_ref, wout_ref, pb_ref, nb_ref,
    out_ref, pn_ref,
    unit_ref, inv_ref, q_ref, k_ref, v_ref, go_ref, qt_ref, kt_ref, got_ref,
    dqt_ref, dk_ref, dv_ref, tok_ref, cot_ref,
):
    scale = HEAD_DIM ** (-0.5)
    take = one_hot(
        lambda o: bits(o, 1, 5) * 8 + bits(o, 7, 1) * 4 + bits(o, 6, 1) * 2 + bits(o, 0, 1)
    )
    for q in range(4):
        rows = move_rows(take, recv_ref[256 * q : 256 * q + 256, :])
        for g in range(2):
            at = 256 * g + 64 * q
            tok_ref[at : at + 64, :] = rows[64 * g : 64 * g + 64]
            cot_ref[at : at + 64, :] = rows[128 + 64 * g : 192 + 64 * g]

    for g in range(2):
        sl = slice(256 * g, 256 * g + 256)
        x = tok_ref[sl, :].astype(F32)
        shifted = x - jnp.mean(x, axis=-1, keepdims=True)
        inv_std = lax.rsqrt(jnp.mean(shifted * shifted, axis=-1, keepdims=True) + NORM_EPS)
        unit = shifted * inv_std
        unit_ref[sl, :] = unit
        inv_ref[sl, :] = jnp.broadcast_to(inv_std, (256, 128))
        normed = (unit * gain_ref[...]).astype(BF16)
        qv = dot_nn(normed, win_ref[:, 0:D]) * scale
        q_ref[sl, :] = qv.astype(BF16)
        qt_ref[D * g : D * g + D, :] = qv.T.astype(BF16)
        kv = dot_nn(normed, win_ref[:, D : 2 * D])
        k_ref[sl, :] = kv.astype(BF16)
        kt_ref[D * g : D * g + D, :] = kv.T.astype(BF16)
        v_ref[sl, :] = dot_nn(normed, win_ref[:, 2 * D : 3 * D]).astype(BF16)
        go = dot_nt(cot_ref[sl, :], wout_ref[...])
        go_ref[sl, :] = go.astype(BF16)
        got_ref[D * g : D * g + D, :] = go.T.astype(BF16)

    row = iota((16, 512), 0)
    lane_in = bits(iota((16, 512), 1), 0, 4)
    ahead = (lane_in + row) < 16

    def head(h, carry):
        hb = lax.shift_right_logical(h, 2)
        hh = lax.bitwise_and(h, 3)
        base = pl.multiple_of(hb * 128, 128)
        mine = lax.shift_right_logical(iota((256, 128), 1), 5) == hh

        line = jnp.where(ahead, pb_ref[pl.ds(h, 1), :], nb_ref[pl.ds(h, 1), :])
        for b in (1, 2, 4, 8):
            line = jnp.where(lax.bitwise_and(row, b) != 0, pltpu.roll(line, b, 1), line)
        turned = [line if r == 0 else pltpu.roll(line, 512 - 16 * r, 1) for r in range(8)]
        bias = jnp.concatenate(
            [
                turned[(15 - i) % 8][:, 128 * ((15 - i) // 8) : 128 * ((15 - i) // 8) + 256]
                for i in range(16)
            ],
            axis=0,
        )
        total = None
        for g in range(2):
            sl = slice(256 * g, 256 * g + 256)
            lanes = pl.ds(base, 128)
            zero = jnp.zeros((256, 128), BF16)
            k_mine = jnp.where(mine, k_ref[sl, lanes], zero)
            v_mine = jnp.where(mine, v_ref[sl, lanes], zero)
            q_mine = jnp.where(mine, q_ref[sl, lanes], zero)
            go_mine = jnp.where(mine, go_ref[sl, lanes], zero)
            tall = pl.ds(pl.multiple_of(D * g + hb * 128, 128), 128)
            thin = pl.ds(pl.multiple_of(D * g + h * 32, 32), 32)
            scores = dot_nn(k_mine, qt_ref[tall, :]) + bias
            top = jnp.max(scores, axis=0, keepdims=True)
            exponent = jnp.exp(scores - top)
            probs = exponent * (1.0 / jnp.sum(exponent, axis=0, keepdims=True))
            grad_probs = dot_nn(v_mine, got_ref[tall, :])
            grad_v = dot_nn(probs.astype(BF16), go_mine)
            dv_ref[sl, lanes] = jnp.where(mine, grad_v.astype(BF16), dv_ref[sl, lanes])
            delta = jnp.sum(probs * grad_probs, axis=0, keepdims=True)
            grad_scores = probs * (grad_probs - delta)
            half = grad_scores.astype(BF16)
            grad_k = dot_nn(half, q_mine)
            dk_ref[sl, lanes] = jnp.where(mine, grad_k.astype(BF16), dk_ref[sl, lanes])
            dqt_ref[thin, :] = dot_nn(kt_ref[thin, :], half) * scale
            total = grad_scores if total is None else total + grad_scores

        fold = None
        blank = jnp.zeros((16, 128), F32)
        for r in range(8):
            a = total[16 * (15 - r) : 16 * (15 - r) + 16]
            b = total[16 * (7 - r) : 16 * (7 - r) + 16]
            wide = jnp.concatenate(
                [a[:, 0:128], a[:, 128:256] + b[:, 0:128], b[:, 128:256], blank], axis=1
            )
            if r:
                wide = pltpu.roll(wide, 16 * r, 1)
            fold = wide if fold is None else fold + wide
        for b in (1, 2, 4, 8):
            fold = jnp.where(lax.bitwise_and(row, b) != 0, pltpu.roll(fold, 512 - b, 1), fold)
        near = jnp.where(ahead, fold, 0.0)
        pn_ref[pl.ds(h, 1), 0:512] = jnp.sum(near, axis=0, keepdims=True)
        pn_ref[pl.ds(h, 1), 512:1024] = jnp.sum(fold - near, axis=0, keepdims=True)
        return carry

    lax.fori_loop(0, HEADS, head, 0)

    for g in range(2):
        sl = slice(256 * g, 256 * g + 256)
        grad_q = dqt_ref[D * g : D * g + D, :].T.astype(BF16)
        grad_normed = (
            dot_nt(grad_q, win_ref[:, 0:D])
            + dot_nt(dk_ref[sl, :], win_ref[:, D : 2 * D])
            + dot_nt(dv_ref[sl, :], win_ref[:, 2 * D : 3 * D])
        )
        grad_unit = grad_normed * gain_ref[...]
        unit = unit_ref[sl, :]
        grad_rows = inv_ref[sl, 0:1] * (
            grad_unit
            - jnp.mean(grad_unit, axis=-1, keepdims=True)
            - unit * jnp.mean(grad_unit * unit, axis=-1, keepdims=True)
        )
        tok_ref[sl, :] = grad_rows.astype(BF16)

    give = one_hot(
        lambda o: bits(o, 1, 1) * 128 + bits(o, 2, 1) * 64 + bits(o, 3, 5) * 2 + bits(o, 0, 1)
    )
    for q in range(4):
        rows = jnp.concatenate(
            [
                tok_ref[256 * g + 64 * q : 256 * g + 64 * q + 64, 256 * half : 256 * half + 256]
                for g in range(2)
                for half in range(2)
            ],
            axis=0,
        )
        out_ref[256 * q : 256 * q + 256, :] = move_rows(give, rows)


def device_index(z, y, x, core):
    return (z * 4 + (y % 2) * 2 + core) * 8 + x * 2 + y // 2


def shift_pairs(axis, step):
    pairs = []
    for z in range(4):
        for y in range(4):
            for x in range(4):
                for core in range(2):
                    there = {"z": z, "y": y, "x": x}
                    there[axis] = (there[axis] + step) % 4
                    pairs.append(
                        (
                            device_index(z, y, x, core),
                            device_index(there["z"], there["y"], there["x"], core),
                        )
                    )
    return pairs


def other_core_pairs():
    return [(i, i ^ 8) for i in range(128)]


def sum_everywhere(part):
    core = lax.rem(lax.axis_index("ha"), 2)
    own = lax.dynamic_slice(part, (8 * core, 0), (8, 1024))
    given = lax.dynamic_slice(part, (8 * (1 - core), 0), (8, 1024))
    own = own + lax.ppermute(given, AXES, other_core_pairs())
    for axis in ("z", "x", "y"):
        one, two, three = (lax.ppermute(own, AXES, shift_pairs(axis, s)) for s in (1, 2, 3))
        own = (own + two) + (one + three)
    other = lax.ppermute(own, AXES, other_core_pairs())
    low = jnp.where(core == 0, own, other)
    high = jnp.where(core == 0, other, own)
    return jnp.concatenate([low, high], axis=0)


def split_bias(bias_table):
    zero = jnp.zeros((HEADS, 1, 16), F32)
    near = jnp.concatenate([bias_table[:, :, 15:31], zero], axis=1)
    far = jnp.pad(bias_table[:, :, 0:15], ((0, 0), (0, 0), (1, 0)))
    far = jnp.concatenate([far[:, 1:31], zero, far[:, 0:1]], axis=1)
    return near.reshape(HEADS, 512), far.reshape(HEADS, 512)


def join_table(part):
    near = part[:, 0:512].reshape(HEADS, 32, 16)[:, 0:31]
    far = part[:, 512:1024].reshape(HEADS, 32, 16)
    far = jnp.concatenate([far[:, 31:32], far[:, 0:30]], axis=1)[:, :, 1:16]
    return jnp.concatenate([far, near], axis=2)


def vmem_specs(count):
    return [pl.BlockSpec(memory_space=pltpu.VMEM)] * count


def body(tokens, cotangent, norm_gain, in_weight, out_weight, bias_table):
    sent = pl.pallas_call(
        pack_kernel,
        out_shape=jax.ShapeDtypeStruct((1024, D), BF16),
        in_specs=vmem_specs(2),
        out_specs=vmem_specs(1)[0],
    )(tokens, cotangent)
    near, far = split_bias(bias_table)
    got = lax.all_to_all(sent.reshape(128, 8, D), AXES, split_axis=0, concat_axis=0, tiled=True)
    back, part = pl.pallas_call(
        group_kernel,
        out_shape=(
            jax.ShapeDtypeStruct((1024, 256), BF16),
            jax.ShapeDtypeStruct((HEADS, 1024), F32),
        ),
        in_specs=vmem_specs(6),
        out_specs=tuple(vmem_specs(2)),
        scratch_shapes=[
            pltpu.VMEM((512, D), F32),
            pltpu.VMEM((512, 128), F32),
            pltpu.VMEM((512, D), BF16),
            pltpu.VMEM((512, D), BF16),
            pltpu.VMEM((512, D), BF16),
            pltpu.VMEM((512, D), BF16),
            pltpu.VMEM((2 * D, 256), BF16),
            pltpu.VMEM((2 * D, 256), BF16),
            pltpu.VMEM((2 * D, 256), BF16),
            pltpu.VMEM((2 * D, 256), F32),
            pltpu.VMEM((512, D), BF16),
            pltpu.VMEM((512, D), BF16),
            pltpu.VMEM((512, D), BF16),
            pltpu.VMEM((512, D), BF16),
        ],
        cost_estimate=pl.CostEstimate(
            flops=20_000_000_000, bytes_accessed=8_000_000, transcendentals=2_000_000
        ),
    )(got.reshape(1024, D), norm_gain.reshape(1, D), in_weight, out_weight, near, far)
    returned = lax.all_to_all(
        back.reshape(128, 8, 256), AXES, split_axis=0, concat_axis=0, tiled=True
    )
    table = join_table(sum_everywhere(part))
    grad_input = pl.pallas_call(
        unpack_kernel,
        out_shape=jax.ShapeDtypeStruct((16, 32, D), BF16),
        in_specs=vmem_specs(1),
        out_specs=vmem_specs(1)[0],
    )(returned.reshape(1024, 256))
    return (grad_input, table)


def solution(mesh):
    in_specs = (P("ha", "wa", None), P("ha", "wa", None), P(), P(), P(), P())
    out_specs = (P("ha", "wa", None), P())
    return jax.shard_map(body, mesh=mesh, in_specs=in_specs, out_specs=out_specs, check_vma=False)
```

time: 332 us -> 108 us (0.33)
  matrix products: 117 us -> 0 us
  local copies, waits for them, and re-layouts: 95.5 us -> 5.76 us
  blocking collectives: 68.6 us -> 0 us
  Pallas kernels: 0 us -> 32.2 us
  waiting for transfers between devices: 9.46 us -> 38.5 us
  other arithmetic: 12.9 us -> 1.13 us
    dot_general x22 -> x0, matrix products: 117 us -> none  [the longest x2 60.8 us: group_grad(): jnp.einsum('haubv,uve->habe', grad_scores.reshape(HEADS, WIN, WIN, WIN, W...]
    psum x1 -> x0, blocking collectives: 68.6 us -> none  [body(): grad_table = lax.psum(jnp.sum(table_parts, axis=0), ('ha', 'wa'))]
    reshape x7 -> x4, local copies, waits for them, and re-layouts: 68.1 us -> 1.77 us  [the longest x2 1.53 us: split_bias(): return (near.reshape(HEADS, 512), far.reshape(HEADS, 512))]
    pallas_call x0 -> x3, Pallas kernels: none -> 32.2 us  [the longest x1 27.4 us: body(): pl.pallas_call(group_kernel, out_shape=(jax.ShapeDtypeStruct((1024, 256),...]
    all_to_all x3 -> x2, waiting for transfers between devices: 9.46 us -> 27.9 us  [the longest x1 17.3 us: body(): lax.all_to_all(sent.reshape(128, 8, D), AXES, split_axis=0, concat_axis=0...]
    ppermute x0 -> x11, waiting for transfers between devices: none -> 10.6 us  [the longest x9 8.52 us: sum_everywhere(): lax.ppermute(own, AXES, shift_pairs(axis, s))]
    ppermute x0 -> x11, starting transfers between devices: none -> 9.34 us  [the longest x9 8.19 us: sum_everywhere(): lax.ppermute(own, AXES, shift_pairs(axis, s))]
    unnamed x23 -> x8, local copies, waits for them, and re-layouts: 9 us -> 2.72 us
  transfers between devices with their start and end apart: 3 -> 13, of which waited for: 1 -> 8; matrix products, arithmetic and copies ran while one was open for 16% -> 3% of each run, Pallas kernels for 0% -> 0%
where the time goes in v1:
time: 108 us
  waiting for transfers between devices  38.5 us (36%)
  Pallas kernels  32.2 us (30%)
  starting transfers between devices  29.4 us (27%)
  local copies, waits for them, and re-layouts  5.76 us (5%)
  other arithmetic  1.13 us (1%)
    pallas_call x1, Pallas kernels, body(): pl.pallas_call(group_kernel, out_shape=(jax.ShapeDtypeStruct((1024, 256),...  27.4 us
    all_to_all x1, waiting for transfers between devices, body(): lax.all_to_all(sent.reshape(128, 8, D), AXES, split_axis=0, concat_axis=0...  17.3 us
    all_to_all x1, starting transfers between devices, body(): lax.all_to_all(sent.reshape(128, 8, D), AXES, split_axis=0, concat_axis=0...  11.5 us
    all_to_all x1, waiting for transfers between devices, body(): lax.all_to_all(back.reshape(128, 8, 256), AXES, split_axis=0, concat_axis...  10.6 us
    all_to_all x1, starting transfers between devices, body(): lax.all_to_all(back.reshape(128, 8, 256), AXES, split_axis=0, concat_axis...  8.53 us
    ppermute x9, waiting for transfers between devices, sum_everywhere(): lax.ppermute(own, AXES, shift_pairs(axis, s))  8.52 us
    ppermute x9, starting transfers between devices, sum_everywhere(): lax.ppermute(own, AXES, shift_pairs(axis, s))  8.19 us
    unnamed x8, local copies, waits for them, and re-layouts  2.72 us
  transfers between devices with their start and end apart: 13, of which 8 were waited for; matrix products, arithmetic and copies ran while one was open for 3% of the time, Pallas kernels for 0%

profile of v1, /device:TPU:1, one launch (start us, length us, event | category | flops | bytes accessed | tf_op | source)
XLA Modules:
  0.0 107.7 jit_solution(835320169038945544)
XLA Ops:
  0.6 2.6 %shard_map.77 = bf16[1024,512]{1,0:T(8,128)(2,1)} custom-call(bf16[16,32,512]{2,1,0:T(8,128)(2,1)} %tok_ref.1, bf16[16,32,512]{2,1,0:T(8,128)(2,1)} %cot_ref.1), custom_call_target="tpu_custom_call" | custom-call | tf_op jit(solution)/shard_map/pallas_call | solution.py:272
  3.3 0.0 copy-start
  3.3 11.5 %all-to-all-start = ((bf16[128,8,512]{2,1,0:T(8,128)(2,1)}), bf16[128,8,512]{2,1,0:T(8,128)(2,1)S(1)}, u32[]{:S(2)}, u32[]{:S(2)}) async-start(bf16[128,8,512]{2,1,0:T(8,128)(2,1)} %bitcast.9), calls=%async_computation | async-start | bytes 2097152 | tf_op jit(solution)/shard_map/all_to_all | solution.py:279
  14.8 0.0 copy-done
  14.8 0.1 slice.30
  14.9 0.1 copy.16
  15.0 0.8 reshape.34.pb_ref
  15.8 0.1 pad.13.clone
  15.9 0.1 pad_slice_fusion
  16.0 0.1 pad_slice_fusion.1
  16.1 0.1 pad_maximum_fusion.1
  16.2 0.1 copy.14
  16.3 0.8 reshape.35.nb_ref
  17.1 17.3 %all-to-all-done = bf16[128,8,512]{2,1,0:T(8,128)(2,1)S(1)} async-done(((bf16[128,8,512]{2,1,0:T(8,128)(2,1)}), bf16[128,8,512]{2,1,0:T(8,128)(2,1)S(1)}, u32[]{:S(2)}, u32[]{:S(2)}) %all-to-all-start) | async-done | bytes 1048608 | tf_op jit(solution)/shard_map/all_to_all | solution.py:279
  34.4 1.0 copy-done.2
  35.3 27.4 %shard_map.78 = (bf16[1024,256]{1,0:T(8,128)(2,1)}, f32[16,1024]{1,0:T(8,128)}) custom-call(bf16[1024,512]{1,0:T(8,128)(2,1)} %bitcast.15, f32[1,512]{1,0:T(1,128)} %bitcast.17, bf16[512,1536]{1,0:T(8,128)(2,1)} %win_ref.1, bf16[512,512]{1,0:T(8,128)(2,1)} %wout_ref.1, f32[16,512]{1,0:T(8,128)} %reshape.34.pb_ref, f32[16,512]{1,0:T(8,128)} %reshape.35.nb_ref), custom_call_target="tpu_custom_call" | custom-call | flops 20000000000 | bytes 8000000 | tf_op jit(solution)/shard_map/pallas_call | solution.py:280
  62.7 0.8 constant_dynamic-slice_fusion
  63.5 0.0 collective-permute-start
  63.5 1.2 %collective-permute-done = f32[8,1024]{1,0:T(8,128)S(1)} collective-permute-done((f32[8,1024]{1,0:T(8,128)S(1)}, f32[8,1024]{1,0:T(8,128)S(1)}, u32[]{:S(2)}, u32[]{:S(2)}) %collective-permute-start) | collective-permute-done | bytes 32800 | tf_op jit(solution)/shard_map/ppermute | solution.py:242
  64.7 0.8 dynamic-slice_add_fusion
  65.5 0.6 collective-permute-start.2
  66.0 2.1 %collective-permute-start.3 = (f32[8,1024]{1,0:T(8,128)S(1)}, f32[8,1024]{1,0:T(8,128)S(1)}, u32[]{:S(2)}, u32[]{:S(2)}) collective-permute-start(f32[8,1024]{1,0:T(8,128)S(1)} %dynamic-slice_add_fusion), channel_id=1, source_target_pairs={{0,96},{8,104},{2,98},{10,106},{4,100},{12,108},{6,102},{14,110},{... | collective-permute-start | bytes 98312 | tf_op jit(solution)/shard_map/ppermute | solution.py:244
  68.2 0.0 collective-permute-start.1
  68.2 1.3 %collective-permute-done.2 = f32[8,1024]{1,0:T(8,128)S(1)} collective-permute-done((f32[8,1024]{1,0:T(8,128)S(1)}, f32[8,1024]{1,0:T(8,128)S(1)}, u32[]{:S(2)}, u32[]{:S(2)}) %collective-permute-start.2) | collective-permute-done | bytes 32800 | tf_op jit(solution)/shard_map/ppermute | solution.py:244
  69.5 0.0 collective-permute-done.3
  69.5 3.0 %collective-permute-done.1 = f32[8,1024]{1,0:T(8,128)S(1)} collective-permute-done((f32[8,1024]{1,0:T(8,128)S(1)}, f32[8,1024]{1,0:T(8,128)S(1)}, u32[]{:S(2)}, u32[]{:S(2)}) %collective-permute-start.1) | collective-permute-done | bytes 32800 | tf_op jit(solution)/shard_map/ppermute | solution.py:244
  72.4 0.3 collective-permute-start.5
  72.7 2.5 %collective-permute-start.6 = (f32[8,1024]{1,0:T(8,128)S(1)}, f32[8,1024]{1,0:T(8,128)S(1)}, u32[]{:S(2)}, u32[]{:S(2)}) collective-permute-start(f32[8,1024]{1,0:T(8,128)S(1)} %add_add_fusion.2), channel_id=1, source_target_pairs={{0,6},{8,14},{2,0},{10,8},{4,2},{12,10},{6,4},{14,12},{16,22},{24,... | collective-permute-start | bytes 98312 | tf_op jit(solution)/shard_map/ppermute | solution.py:244
  75.2 0.0 collective-permute-start.4
  75.2 1.3 %collective-permute-done.5 = f32[8,1024]{1,0:T(8,128)S(1)} collective-permute-done((f32[8,1024]{1,0:T(8,128)S(1)}, f32[8,1024]{1,0:T(8,128)S(1)}, u32[]{:S(2)}, u32[]{:S(2)}) %collective-permute-start.5) | collective-permute-done | bytes 32800 | tf_op jit(solution)/shard_map/ppermute | solution.py:244
  76.5 0.0 collective-permute-done.6
  76.5 3.0 %collective-permute-done.4 = f32[8,1024]{1,0:T(8,128)S(1)} collective-permute-done((f32[8,1024]{1,0:T(8,128)S(1)}, f32[8,1024]{1,0:T(8,128)S(1)}, u32[]{:S(2)}, u32[]{:S(2)}) %collective-permute-start.4) | collective-permute-done | bytes 32800 | tf_op jit(solution)/shard_map/ppermute | solution.py:244
  79.5 0.4 collective-permute-start.8
  79.9 2.3 %collective-permute-start.9 = (f32[8,1024]{1,0:T(8,128)S(1)}, f32[8,1024]{1,0:T(8,128)S(1)}, u32[]{:S(2)}, u32[]{:S(2)}) collective-permute-start(f32[8,1024]{1,0:T(8,128)S(1)} %add_add_fusion.1), channel_id=1, source_target_pairs={{0,17},{8,25},{2,19},{10,27},{4,21},{12,29},{6,23},{14,31},{16,0},... | collective-permute-start | bytes 98312 | tf_op jit(solution)/shard_map/ppermute | solution.py:244
  82.2 0.0 collective-permute-start.7
  82.2 8.5 %all-to-all-start.1 = ((bf16[128,8,256]{2,1,0:T(8,128)(2,1)}), bf16[128,8,256]{2,1,0:T(8,128)(2,1)S(1)}, u32[]{:S(2)}, u32[]{:S(2)}) async-start(bf16[128,8,256]{2,1,0:T(8,128)(2,1)} %bitcast.16), calls=%async_computation.1 | async-start | bytes 1048576 | tf_op jit(solution)/shard_map/all_to_all | solution.py:308
  90.8 0.0 collective-permute-done.8
  90.8 0.0 collective-permute-done.9
  90.8 0.0 collective-permute-done.7
  90.8 1.1 %collective-permute-start.10 = (f32[8,1024]{1,0:T(8,128)S(1)}, f32[8,1024]{1,0:T(8,128)S(1)}, u32[]{:S(2)}, u32[]{:S(2)}) collective-permute-start(f32[8,1024]{1,0:T(8,128)S(1)} %add_add_fusion), channel_id=1, source_target_pairs={{0,8},{1,9},{2,10},{3,11},{4,12},{5,13},{6,14},{7,15},{8,0},{9,1},... | collective-permute-start | bytes 98312 | tf_op jit(solution)/shard_map/ppermute | solution.py:246
  92.0 0.9 collective-permute-done.10
  92.8 0.1 reshape.38
  93.0 0.1 reshape.39
  93.1 0.2 fusion
  93.3 0.8 copy.15
  94.2 10.6 %all-to-all-done.1 = bf16[128,8,256]{2,1,0:T(8,128)(2,1)S(1)} async-done(((bf16[128,8,256]{2,1,0:T(8,128)(2,1)}), bf16[128,8,256]{2,1,0:T(8,128)(2,1)S(1)}, u32[]{:S(2)}, u32[]{:S(2)}) %all-to-all-start.1) | async-done | bytes 524320 | tf_op jit(solution)/shard_map/all_to_all | solution.py:308
  104.8 0.8 copy-done.1
  105.6 2.1 %shard_map.79 = bf16[16,32,512]{2,1,0:T(8,128)(2,1)} custom-call(bf16[1024,256]{1,0:T(8,128)(2,1)} %bitcast.12), custom_call_target="tpu_custom_call" | custom-call | tf_op jit(solution)/shard_map/pallas_call | solution.py:312
  (9 shorter events, 0.1 us)
Async XLA Ops:
  3.3 11.5 %copy-start = (f32[16,31,31]{2,0,1:T(8,128)S(1)}, f32[16,31,31]{2,0,1:T(8,128)}, u32[]{:S(2)}) copy-start(f32[16,31,31]{2,0,1:T(8,128)} %param.11) | copy-start | bytes 184516
  3.3 31.1 %all-to-all-start = ((bf16[128,8,512]{2,1,0:T(8,128)(2,1)}), bf16[128,8,512]{2,1,0:T(8,128)(2,1)S(1)}, u32[]{:S(2)}, u32[]{:S(2)}) async-start(bf16[128,8,512]{2,1,0:T(8,128)(2,1)} %bitcast.9), calls=%async_computation | async-start | bytes 2097152 | tf_op jit(solution)/shard_map/all_to_all | solution.py:279
  34.4 1.0 copy-start.2
  63.5 1.2 %collective-permute-start = (f32[8,1024]{1,0:T(8,128)S(1)}, f32[8,1024]{1,0:T(8,128)S(1)}, u32[]{:S(2)}, u32[]{:S(2)}) collective-permute-start(f32[8,1024]{1,0:T(8,128)S(1)} %constant_dynamic-slice_fusion), channel_id=1, source_target_pairs={{0,8},{1,9},{2,10},{3,11},{4,12},{5,13},{6,14},{7,15},{8,0},{9,1},... | collective-permute-start | bytes 98312 | tf_op jit(solution)/shard_map/ppermute | solution.py:242
  65.5 4.0 %collective-permute-start.2 = (f32[8,1024]{1,0:T(8,128)S(1)}, f32[8,1024]{1,0:T(8,128)S(1)}, u32[]{:S(2)}, u32[]{:S(2)}) collective-permute-start(f32[8,1024]{1,0:T(8,128)S(1)} %dynamic-slice_add_fusion), channel_id=1, source_target_pairs={{0,32},{8,40},{2,34},{10,42},{4,36},{12,44},{6,38},{14,46},{16,48}... | collective-permute-start | bytes 98312 | tf_op jit(solution)/shard_map/ppermute | solution.py:244
  66.0 3.4 %collective-permute-start.3 = (f32[8,1024]{1,0:T(8,128)S(1)}, f32[8,1024]{1,0:T(8,128)S(1)}, u32[]{:S(2)}, u32[]{:S(2)}) collective-permute-start(f32[8,1024]{1,0:T(8,128)S(1)} %dynamic-slice_add_fusion), channel_id=1, source_target_pairs={{0,96},{8,104},{2,98},{10,106},{4,100},{12,108},{6,102},{14,110},{... | collective-permute-start | bytes 98312 | tf_op jit(solution)/shard_map/ppermute | solution.py:244
  68.2 4.3 %collective-permute-start.1 = (f32[8,1024]{1,0:T(8,128)S(1)}, f32[8,1024]{1,0:T(8,128)S(1)}, u32[]{:S(2)}, u32[]{:S(2)}) collective-permute-start(f32[8,1024]{1,0:T(8,128)S(1)} %dynamic-slice_add_fusion), channel_id=1, source_target_pairs={{0,64},{8,72},{2,66},{10,74},{4,68},{12,76},{6,70},{14,78},{16,80}... | collective-permute-start | bytes 98312 | tf_op jit(solution)/shard_map/ppermute | solution.py:244
  72.4 4.0 %collective-permute-start.5 = (f32[8,1024]{1,0:T(8,128)S(1)}, f32[8,1024]{1,0:T(8,128)S(1)}, u32[]{:S(2)}, u32[]{:S(2)}) collective-permute-start(f32[8,1024]{1,0:T(8,128)S(1)} %add_add_fusion.2), channel_id=1, source_target_pairs={{0,2},{8,10},{2,4},{10,12},{4,6},{12,14},{6,0},{14,8},{16,18},{24,... | collective-permute-start | bytes 98312 | tf_op jit(solution)/shard_map/ppermute | solution.py:244
  72.7 3.8 %collective-permute-start.6 = (f32[8,1024]{1,0:T(8,128)S(1)}, f32[8,1024]{1,0:T(8,128)S(1)}, u32[]{:S(2)}, u32[]{:S(2)}) collective-permute-start(f32[8,1024]{1,0:T(8,128)S(1)} %add_add_fusion.2), channel_id=1, source_target_pairs={{0,6},{8,14},{2,0},{10,8},{4,2},{12,10},{6,4},{14,12},{16,22},{24,... | collective-permute-start | bytes 98312 | tf_op jit(solution)/shard_map/ppermute | solution.py:244
  75.2 4.3 %collective-permute-start.4 = (f32[8,1024]{1,0:T(8,128)S(1)}, f32[8,1024]{1,0:T(8,128)S(1)}, u32[]{:S(2)}, u32[]{:S(2)}) collective-permute-start(f32[8,1024]{1,0:T(8,128)S(1)} %add_add_fusion.2), channel_id=1, source_target_pairs={{0,4},{8,12},{2,6},{10,14},{4,0},{12,8},{6,2},{14,10},{16,20},{24,... | collective-permute-start | bytes 98312 | tf_op jit(solution)/shard_map/ppermute | solution.py:244
  79.5 11.3 %collective-permute-start.8 = (f32[8,1024]{1,0:T(8,128)S(1)}, f32[8,1024]{1,0:T(8,128)S(1)}, u32[]{:S(2)}, u32[]{:S(2)}) collective-permute-start(f32[8,1024]{1,0:T(8,128)S(1)} %add_add_fusion.1), channel_id=1, source_target_pairs={{0,16},{8,24},{2,18},{10,26},{4,20},{12,28},{6,22},{14,30},{16,1},... | collective-permute-start | bytes 98312 | tf_op jit(solution)/shard_map/ppermute | solution.py:244
  79.9 10.9 %collective-permute-start.9 = (f32[8,1024]{1,0:T(8,128)S(1)}, f32[8,1024]{1,0:T(8,128)S(1)}, u32[]{:S(2)}, u32[]{:S(2)}) collective-permute-start(f32[8,1024]{1,0:T(8,128)S(1)} %add_add_fusion.1), channel_id=1, source_target_pairs={{0,17},{8,25},{2,19},{10,27},{4,21},{12,29},{6,23},{14,31},{16,0},... | collective-permute-start | bytes 98312 | tf_op jit(solution)/shard_map/ppermute | solution.py:244
  82.2 8.6 %collective-permute-start.7 = (f32[8,1024]{1,0:T(8,128)S(1)}, f32[8,1024]{1,0:T(8,128)S(1)}, u32[]{:S(2)}, u32[]{:S(2)}) collective-permute-start(f32[8,1024]{1,0:T(8,128)S(1)} %add_add_fusion.1), channel_id=1, source_target_pairs={{0,1},{8,9},{2,3},{10,11},{4,5},{12,13},{6,7},{14,15},{16,17},{24,... | collective-permute-start | bytes 98312 | tf_op jit(solution)/shard_map/ppermute | solution.py:244
  82.2 22.6 %all-to-all-start.1 = ((bf16[128,8,256]{2,1,0:T(8,128)(2,1)}), bf16[128,8,256]{2,1,0:T(8,128)(2,1)S(1)}, u32[]{:S(2)}, u32[]{:S(2)}) async-start(bf16[128,8,256]{2,1,0:T(8,128)(2,1)} %bitcast.16), calls=%async_computation.1 | async-start | bytes 1048576 | tf_op jit(solution)/shard_map/all_to_all | solution.py:308
  90.8 2.0 %collective-permute-start.10 = (f32[8,1024]{1,0:T(8,128)S(1)}, f32[8,1024]{1,0:T(8,128)S(1)}, u32[]{:S(2)}, u32[]{:S(2)}) collective-permute-start(f32[8,1024]{1,0:T(8,128)S(1)} %add_add_fusion), channel_id=1, source_target_pairs={{0,8},{1,9},{2,10},{3,11},{4,12},{5,13},{6,14},{7,15},{8,0},{9,1},... | collective-permute-start | bytes 98312 | tf_op jit(solution)/shard_map/ppermute | solution.py:246
  104.8 0.8 copy-start.1

commit v2 on v1

v2 whole, which is shorter than its diff:
```python
import jax
import jax.numpy as jnp
from jax import lax
from jax.experimental import pallas as pl
from jax.experimental.pallas import tpu as pltpu
from jax.sharding import PartitionSpec as P

D = 512
HEADS = 16
HEAD_DIM = 32
NORM_EPS = 1e-05
AXES = ("ha", "wa")
BF16 = jnp.bfloat16
F32 = jnp.float32
SMALL_GRANT = 12 << 20
LARGE_GRANT = 50 << 20


def iota(shape, dim):
    return lax.broadcasted_iota(jnp.int32, shape, dim)


def bits(x, low, count):
    return lax.bitwise_and(lax.shift_right_logical(x, low), (1 << count) - 1)


def one_hot(source):
    o = iota((256, 256), 0)
    return jnp.where(source(o) == iota((256, 256), 1), 1.0, 0.0).astype(BF16)


def move_rows(matrix, rows):
    return jnp.dot(matrix, rows, preferred_element_type=F32).astype(BF16)


def pack_kernel(tok_hbm, cot_hbm, out_hbm, rows_in, rows_out, in_sem, out_sem):
    def fetch(q, kind):
        source = (tok_hbm, cot_hbm)[kind]
        return pltpu.make_async_copy(
            source.at[pl.ds(4 * q, 4)], rows_in.at[q, kind], in_sem.at[q, kind]
        )

    def emit(q):
        return pltpu.make_async_copy(
            rows_out.at[pl.ds(256 * q, 256)], out_hbm.at[pl.ds(256 * q, 256)], out_sem.at[q]
        )

    for q in range(4):
        fetch(q, 0).start()
        fetch(q, 1).start()
    perm = one_hot(
        lambda o: bits(o, 2, 1) * 128
        + bits(o, 6, 2) * 32
        + bits(o, 0, 1) * 16
        + bits(o, 3, 3) * 2
        + bits(o, 1, 1)
    )
    for q in range(4):
        fetch(q, 0).wait()
        fetch(q, 1).wait()
        rows_out[256 * q : 256 * q + 256, :] = move_rows(perm, rows_in[q].reshape(256, D))
        emit(q).start()
    for q in range(4):
        emit(q).wait()


def unpack_kernel(in_ref, out_ref):
    perm = one_hot(
        lambda o: bits(o, 5, 2) * 64
        + bits(o, 1, 3) * 8
        + bits(o, 7, 1) * 4
        + bits(o, 0, 1) * 2
        + bits(o, 4, 1)
    )
    for q in range(4):
        rows = move_rows(perm, in_ref[256 * q : 256 * q + 256, :])
        out_ref[4 * q : 4 * q + 4, :, 0:256] = rows[0:128].reshape(4, 32, 256)
        out_ref[4 * q : 4 * q + 4, :, 256:512] = rows[128:256].reshape(4, 32, 256)


def dot_nn(a, b):
    return jnp.dot(a, b, preferred_element_type=F32)


def prep_kernel(near_ref, far_ref, win_ref, wout_ref, bias_ref, win_t_ref, wout_t_ref):
    row = iota((16, 512), 0)
    ahead = (bits(iota((16, 512), 1), 0, 4) + row) < 16

    def head(h, carry):
        line = jnp.where(ahead, near_ref[pl.ds(h, 1), :], far_ref[pl.ds(h, 1), :])
        for b in (1, 2, 4, 8):
            line = jnp.where(lax.bitwise_and(row, b) != 0, pltpu.roll(line, b, 1), line)
        for r in range(8):
            turned = line if r == 0 else pltpu.roll(line, 512 - 16 * r, 1)
            bias_ref[h, 16 * (15 - r) : 16 * (15 - r) + 16, :] = turned[:, 0:256]
            bias_ref[h, 16 * (7 - r) : 16 * (7 - r) + 16, :] = turned[:, 128:384]
        return carry

    lax.fori_loop(0, HEADS, head, 0)
    for part in range(3):
        cols = slice(D * part, D * part + D)
        win_t_ref[cols, :] = win_ref[:, cols].astype(F32).T.astype(BF16)
    wout_t_ref[...] = wout_ref[...].astype(F32).T.astype(BF16)


def group_kernel(
    recv_ref, gain_ref, win_ref, win_t_hbm, wout_t_hbm, bias_hbm,
    out_ref, pn_ref,
    unit_ref, inv_ref, q_ref, k_ref, v_ref, go_ref, qt_ref, kt_ref, got_ref,
    dqt_ref, dk_ref, dv_ref, tok_ref, cot_ref, dk_part, dv_part,
    win_t_ref, wout_t_ref, bias_ref, weight_sem, bias_sem,
):
    scale = HEAD_DIM ** (-0.5)
    fetch_out = pltpu.make_async_copy(wout_t_hbm, wout_t_ref, weight_sem.at[0])
    fetch_in = pltpu.make_async_copy(win_t_hbm, win_t_ref, weight_sem.at[1])

    def fetch_bias(hb):
        four = pl.ds(4 * hb, 4)
        return pltpu.make_async_copy(bias_hbm.at[four], bias_ref.at[four], bias_sem.at[hb])

    fetch_out.start()
    for hb in range(4):
        fetch_bias(hb).start()
    fetch_in.start()
    take = one_hot(
        lambda o: bits(o, 1, 5) * 8 + bits(o, 7, 1) * 4 + bits(o, 6, 1) * 2 + bits(o, 0, 1)
    )
    for q in range(4):
        rows = move_rows(take, recv_ref[256 * q : 256 * q + 256, :])
        for g in range(2):
            at = 256 * g + 64 * q
            tok_ref[at : at + 64, :] = rows[64 * g : 64 * g + 64]
            cot_ref[at : at + 64, :] = rows[128 + 64 * g : 192 + 64 * g]

    for g in range(2):
        sl = slice(256 * g, 256 * g + 256)
        x = tok_ref[sl, :].astype(F32)
        shifted = x - jnp.mean(x, axis=-1, keepdims=True)
        inv_std = lax.rsqrt(jnp.mean(shifted * shifted, axis=-1, keepdims=True) + NORM_EPS)
        unit = shifted * inv_std
        unit_ref[sl, :] = unit
        inv_ref[sl, :] = jnp.broadcast_to(inv_std, (256, 128))
        normed = (unit * gain_ref[...]).astype(BF16)
        qv = dot_nn(normed, win_ref[:, 0:D]) * scale
        q_ref[sl, :] = qv.astype(BF16)
        qt_ref[D * g : D * g + D, :] = qv.T.astype(BF16)
        kv = dot_nn(normed, win_ref[:, D : 2 * D])
        k_ref[sl, :] = kv.astype(BF16)
        kt_ref[D * g : D * g + D, :] = kv.T.astype(BF16)
        v_ref[sl, :] = dot_nn(normed, win_ref[:, 2 * D : 3 * D]).astype(BF16)
        if g == 0:
            fetch_out.wait()
        go = dot_nn(cot_ref[sl, :], wout_t_ref[...])
        go_ref[sl, :] = go.astype(BF16)
        got_ref[D * g : D * g + D, :] = go.T.astype(BF16)

    row = iota((16, 512), 0)
    ahead = (bits(iota((16, 512), 1), 0, 4) + row) < 16
    owner = lax.shift_right_logical(iota((256, 128), 1), 5)

    def only(rows, hh):
        pieces = [jnp.zeros((32 * hh, 256), BF16)] if hh else []
        pieces.append(rows)
        if hh < 3:
            pieces.append(jnp.zeros((96 - 32 * hh, 256), BF16))
        return jnp.concatenate(pieces, axis=0)

    def block(hb, carry):
        lanes = pl.ds(pl.multiple_of(hb * 128, 128), 128)
        fetch_bias(hb).wait()

        def thin(g, hh):
            return pl.ds(pl.multiple_of(D * g + hb * 128 + 32 * hh, 32), 32)

        def forward(hh, g):
            sl = slice(256 * g, 256 * g + 256)
            scores = dot_nn(k_ref[sl, lanes], only(qt_ref[thin(g, hh), :], hh))
            grad_probs = dot_nn(v_ref[sl, lanes], only(got_ref[thin(g, hh), :], hh))
            return scores, grad_probs

        def backward(hh, g, scores, grad_probs):
            sl = slice(256 * g, 256 * g + 256)
            probs_half, scores_half, grads = [], [], []
            for t in (slice(0, 128), slice(128, 256)):
                shifted = scores[:, t] + bias_ref[hb * 4 + hh, :, t]
                exponent = jnp.exp(shifted - jnp.max(shifted, axis=0, keepdims=True))
                probs = exponent * (1.0 / jnp.sum(exponent, axis=0, keepdims=True))
                probs_half.append(probs.astype(BF16))
                delta = jnp.sum(probs * grad_probs[:, t], axis=0, keepdims=True)
                grad = probs * (grad_probs[:, t] - delta)
                scores_half.append(grad.astype(BF16))
                grads.append(grad)
            half = jnp.concatenate(scores_half, axis=1)
            mine = owner == hh
            grad_v = dot_nn(jnp.concatenate(probs_half, axis=1), go_ref[sl, lanes])
            pltpu.store(dv_part.at[sl, :], grad_v, mask=mine)
            pltpu.store(dk_part.at[sl, :], dot_nn(half, q_ref[sl, lanes]), mask=mine)
            dqt_ref[thin(g, hh), :] = dot_nn(kt_ref[thin(g, hh), :], half) * scale
            return grads

        units = [(hh, g) for hh in range(4) for g in range(2)]
        ready = forward(*units[0])
        total = None
        for n, (hh, g) in enumerate(units):
            after = forward(*units[n + 1]) if n + 1 < len(units) else None
            grads = backward(hh, g, *ready)
            ready = after
            if g == 0:
                total = grads
                continue
            left, right = total[0] + grads[0], total[1] + grads[1]
            fold = None
            blank = jnp.zeros((16, 128), F32)
            for r in range(8):
                a = slice(16 * (15 - r), 16 * (15 - r) + 16)
                b = slice(16 * (7 - r), 16 * (7 - r) + 16)
                wide = jnp.concatenate([left[a], right[a] + left[b], right[b], blank], axis=1)
                if r:
                    wide = pltpu.roll(wide, 16 * r, 1)
                fold = wide if fold is None else fold + wide
            for b in (1, 2, 4, 8):
                fold = jnp.where(lax.bitwise_and(row, b) != 0, pltpu.roll(fold, 512 - b, 1), fold)
            near = jnp.where(ahead, fold, 0.0)
            h = hb * 4 + hh
            pn_ref[pl.ds(h, 1), 0:512] = jnp.sum(near, axis=0, keepdims=True)
            pn_ref[pl.ds(h, 1), 512:1024] = jnp.sum(fold - near, axis=0, keepdims=True)
        dk_ref[:, lanes] = dk_part[...].astype(BF16)
        dv_ref[:, lanes] = dv_part[...].astype(BF16)
        return carry

    lax.fori_loop(0, 4, block, 0)
    fetch_in.wait()

    for g in range(2):
        sl = slice(256 * g, 256 * g + 256)
        grad_q = dqt_ref[D * g : D * g + D, :].T.astype(BF16)
        grad_normed = (
            dot_nn(grad_q, win_t_ref[0:D, :])
            + dot_nn(dk_ref[sl, :], win_t_ref[D : 2 * D, :])
            + dot_nn(dv_ref[sl, :], win_t_ref[2 * D : 3 * D, :])
        )
        grad_unit = grad_normed * gain_ref[...]
        unit = unit_ref[sl, :]
        grad_rows = inv_ref[sl, 0:1] * (
            grad_unit
            - jnp.mean(grad_unit, axis=-1, keepdims=True)
            - unit * jnp.mean(grad_unit * unit, axis=-1, keepdims=True)
        )
        tok_ref[sl, :] = grad_rows.astype(BF16)

    give = one_hot(
        lambda o: bits(o, 1, 1) * 128 + bits(o, 2, 1) * 64 + bits(o, 3, 5) * 2 + bits(o, 0, 1)
    )
    for q in range(4):
        rows = jnp.concatenate(
            [
                tok_ref[256 * g + 64 * q : 256 * g + 64 * q + 64, 256 * half : 256 * half + 256]
                for g in range(2)
                for half in range(2)
            ],
            axis=0,
        )
        out_ref[256 * q : 256 * q + 256, :] = move_rows(give, rows)


def device_index(z, y, x, core):
    return (z * 4 + (y % 2) * 2 + core) * 8 + x * 2 + y // 2


def shift_pairs(axis, step):
    pairs = []
    for z in range(4):
        for y in range(4):
            for x in range(4):
                for core in range(2):
                    there = {"z": z, "y": y, "x": x}
                    there[axis] = (there[axis] + step) % 4
                    pairs.append(
                        (
                            device_index(z, y, x, core),
                            device_index(there["z"], there["y"], there["x"], core),
                        )
                    )
    return pairs


def other_core_pairs():
    return [(i, i ^ 8) for i in range(128)]


def sum_everywhere(part):
    core = lax.rem(lax.axis_index("ha"), 2)
    own = lax.dynamic_slice(part, (8 * core, 0), (8, 1024))
    given = lax.dynamic_slice(part, (8 * (1 - core), 0), (8, 1024))
    got = lax.ppermute(given, AXES, other_core_pairs())
    own = own + got
    for axis in ("z", "x", "y"):
        one, two, three = (lax.ppermute(own, AXES, shift_pairs(axis, s)) for s in (1, 2, 3))
        own = (own + two) + (one + three)
    other = lax.ppermute(own, AXES, other_core_pairs())
    low = jnp.where(core == 0, own, other)
    high = jnp.where(core == 0, other, own)
    return jnp.concatenate([low, high], axis=0)


def split_bias(bias_table):
    zero = jnp.zeros((HEADS, 1, 16), F32)
    near = jnp.concatenate([bias_table[:, :, 15:31], zero], axis=1)
    far = jnp.pad(bias_table[:, :, 0:15], ((0, 0), (0, 0), (1, 0)))
    far = jnp.concatenate([far[:, 1:31], zero, far[:, 0:1]], axis=1)
    return near.reshape(HEADS, 512), far.reshape(HEADS, 512)


def join_table(part):
    near = part[:, 0:512].reshape(HEADS, 32, 16)[:, 0:31]
    far = part[:, 512:1024].reshape(HEADS, 32, 16)
    far = jnp.concatenate([far[:, 31:32], far[:, 0:30]], axis=1)[:, :, 1:16]
    return jnp.concatenate([far, near], axis=2)


def vmem_specs(count):
    return [pl.BlockSpec(memory_space=pltpu.VMEM)] * count


def step(tokens, cotangent, norm_gain, in_weight, out_weight, bias_table):
    sent = pl.pallas_call(
        pack_kernel,
        out_shape=jax.ShapeDtypeStruct((1024, D), BF16),
        in_specs=[pl.BlockSpec(memory_space=pl.ANY)] * 2,
        out_specs=pl.BlockSpec(memory_space=pl.ANY),
        scratch_shapes=[
            pltpu.VMEM((4, 2, 4, 32, D), BF16),
            pltpu.VMEM((1024, D), BF16),
            pltpu.SemaphoreType.DMA((4, 2)),
            pltpu.SemaphoreType.DMA((4,)),
        ],
    )(tokens, cotangent)
    near, far = split_bias(bias_table)
    got = lax.all_to_all(sent.reshape(128, 8, D), AXES, split_axis=0, concat_axis=0, tiled=True)
    bias, in_turned, out_turned = pl.pallas_call(
        prep_kernel,
        out_shape=(
            jax.ShapeDtypeStruct((HEADS, 256, 256), F32),
            jax.ShapeDtypeStruct((3 * D, D), BF16),
            jax.ShapeDtypeStruct((D, D), BF16),
        ),
        in_specs=vmem_specs(4),
        out_specs=tuple(vmem_specs(3)),
        compiler_params=pltpu.CompilerParams(vmem_limit_bytes=LARGE_GRANT),
    )(near, far, in_weight, out_weight)
    back, part = pl.pallas_call(
        group_kernel,
        out_shape=(
            jax.ShapeDtypeStruct((1024, 256), BF16),
            jax.ShapeDtypeStruct((HEADS, 1024), F32),
        ),
        in_specs=vmem_specs(3) + [pl.BlockSpec(memory_space=pltpu.HBM)] * 3,
        out_specs=tuple(vmem_specs(2)),
        scratch_shapes=[
            pltpu.VMEM((512, D), F32),
            pltpu.VMEM((512, 128), F32),
            pltpu.VMEM((512, D), BF16),
            pltpu.VMEM((512, D), BF16),
            pltpu.VMEM((512, D), BF16),
            pltpu.VMEM((512, D), BF16),
            pltpu.VMEM((2 * D, 256), BF16),
            pltpu.VMEM((2 * D, 256), BF16),
            pltpu.VMEM((2 * D, 256), BF16),
            pltpu.VMEM((2 * D, 256), F32),
            pltpu.VMEM((512, D), BF16),
            pltpu.VMEM((512, D), BF16),
            pltpu.VMEM((512, D), BF16),
            pltpu.VMEM((512, D), BF16),
            pltpu.VMEM((512, 128), F32),
            pltpu.VMEM((512, 128), F32),
            pltpu.VMEM((3 * D, D), BF16),
            pltpu.VMEM((D, D), BF16),
            pltpu.VMEM((HEADS, 256, 256), F32),
            pltpu.SemaphoreType.DMA((2,)),
            pltpu.SemaphoreType.DMA((4,)),
        ],
        compiler_params=pltpu.CompilerParams(vmem_limit_bytes=LARGE_GRANT),
        cost_estimate=pl.CostEstimate(
            flops=20_000_000_000, bytes_accessed=8_000_000, transcendentals=2_000_000
        ),
    )(got.reshape(1024, D), norm_gain.reshape(1, D), in_weight, in_turned, out_turned, bias)
    returned = lax.all_to_all(
        back.reshape(128, 8, 256), AXES, split_axis=0, concat_axis=0, tiled=True
    )
    table = join_table(sum_everywhere(part))
    grad_input = pl.pallas_call(
        unpack_kernel,
        out_shape=jax.ShapeDtypeStruct((16, 32, D), BF16),
        in_specs=vmem_specs(1),
        out_specs=vmem_specs(1)[0],
        compiler_params=pltpu.CompilerParams(vmem_limit_bytes=SMALL_GRANT),
    )(returned.reshape(1024, 256))
    return (grad_input, table)


def solution(mesh):
    in_specs = (P("ha", "wa", None), P("ha", "wa", None), P(), P(), P(), P())
    out_specs = (P("ha", "wa", None), P())
    return jax.shard_map(step, mesh=mesh, in_specs=in_specs, out_specs=out_specs, check_vma=False)
```

time: 108 us -> 91.2 us (0.84)
  waiting for transfers between devices: 38.5 us -> 27.1 us
  Pallas kernels: 32.2 us -> 27.8 us
    all_to_all x2, waiting for transfers between devices: 27.9 us -> 16.6 us  [the longest x1 10.6 us: step(): lax.all_to_all(back.reshape(128, 8, 256), AXES, split_axis=0, concat_axis...]
    pallas_call x3 -> x4, Pallas kernels: 32.2 us -> 27.8 us  [the longest x1 13.6 us: step(): pl.pallas_call(group_kernel, out_shape=(jax.ShapeDtypeStruct((1024, 256),...]
    unnamed x8 -> x16, local copies, waits for them, and re-layouts: 2.72 us -> 4.15 us
    reshape x2, local copies, waits for them, and re-layouts: 1.53 us -> 0.31 us  [split_bias(): return (near.reshape(HEADS, 512), far.reshape(HEADS, 512))]
  transfers between devices with their start and end apart: 13 -> 13, of which waited for: 8 -> 8; matrix products, arithmetic and copies ran while one was open for 3% -> 3% of each run, Pallas kernels for 0% -> 11%
where the time goes in v2:
time: 91.2 us; the launch traced here: 90.9 us
  starting transfers between devices  29.4 us (32%)
  Pallas kernels  27.8 us (30%)
  waiting for transfers between devices  27.1 us (30%)
  local copies, waits for them, and re-layouts  5.22 us (6%)
    pallas_call x1, Pallas kernels, step(): pl.pallas_call(group_kernel, out_shape=(jax.ShapeDtypeStruct((1024, 256),...  13.6 us
    all_to_all x1, starting transfers between devices, step(): lax.all_to_all(sent.reshape(128, 8, D), AXES, split_axis=0, concat_axis=0...  11.5 us
    all_to_all x1, waiting for transfers between devices, step(): lax.all_to_all(back.reshape(128, 8, 256), AXES, split_axis=0, concat_axis...  10.6 us
    pallas_call x1, Pallas kernels, step(): pl.pallas_call(prep_kernel, out_shape=(jax.ShapeDtypeStruct((HEADS, 256,...  10.4 us
    all_to_all x1, starting transfers between devices, step(): lax.all_to_all(back.reshape(128, 8, 256), AXES, split_axis=0, concat_axis...  8.53 us
    ppermute x9, waiting for transfers between devices, sum_everywhere(): lax.ppermute(own, AXES, shift_pairs(axis, s))  8.53 us
    ppermute x9, starting transfers between devices, sum_everywhere(): lax.ppermute(own, AXES, shift_pairs(axis, s))  8.18 us
    all_to_all x1, waiting for transfers between devices, step(): lax.all_to_all(sent.reshape(128, 8, D), AXES, split_axis=0, concat_axis=0...  5.94 us
  transfers between devices with their start and end apart: 13, of which 8 were waited for; matrix products, arithmetic and copies ran while one was open for 3% of the time, Pallas kernels for 11%

profile of v2, /device:TPU:1, one launch (start us, length us, event | category | flops | bytes accessed | tf_op | source)
XLA Modules:
  0.0 90.9 jit_solution(6758148558274948784)
XLA Ops:
  0.6 2.7 %shard_map.77 = bf16[1024,512]{1,0:T(8,128)(2,1)} custom-call(bf16[16,32,512]{2,1,0:T(8,128)(2,1)} %tok_hbm.1, bf16[16,32,512]{2,1,0:T(8,128)(2,1)} %cot_hbm.1), custom_call_target="tpu_custom_call" | custom-call | tf_op jit(solution)/shard_map/pallas_call | solution.py:326
  3.3 0.0 copy-start.6
  3.4 11.5 %all-to-all-start = ((bf16[128,8,512]{2,1,0:T(8,128)(2,1)}), bf16[128,8,512]{2,1,0:T(8,128)(2,1)S(1)}, u32[]{:S(2)}, u32[]{:S(2)}) async-start(bf16[128,8,512]{2,1,0:T(8,128)(2,1)} %bitcast.12), calls=%async_computation | async-start | bytes 2097152 | tf_op jit(solution)/shard_map/all_to_all | solution.py:339
  14.9 0.1 slice.30
  15.0 0.1 copy.16
  15.1 0.0 copy-start.1
  15.1 0.2 reshape.34.near_ref
  15.3 0.1 pad.13.clone
  15.4 0.1 pad_slice_fusion
  15.5 0.1 pad_slice_fusion.1
  15.6 0.1 pad_maximum_fusion.1
  15.7 0.0 copy-start
  15.7 0.0 copy-start.5
  15.7 0.1 copy.14
  15.8 0.2 reshape.35.far_ref
  16.0 0.2 copy-done.1
  16.2 10.4 %shard_map.78 = (f32[16,256,256]{2,1,0:T(8,128)}, bf16[1536,512]{1,0:T(8,128)(2,1)S(1)}, bf16[512,512]{1,0:T(8,128)(2,1)S(1)}) custom-call(f32[16,512]{1,0:T(8,128)S(1)} %reshape.34.near_ref, f32[16,512]{1,0:T(8,128)S(1)} %reshape.35.far_ref, bf16[512,1536]{1,0:T(8,128)(2,1)} %win_ref.3, bf16[512,512]{1,0:T(8,128)(2,1)S(1)} %copy-done.1), custom_call_target="tpu_custom_call" | custom-call | tf_op jit(solution)/shard_map/pallas_call | solution.py:340
  26.5 1.2 %copy-done.2 = bf16[1536,512]{1,0:T(8,128)(2,1)} copy-done((bf16[1536,512]{1,0:T(8,128)(2,1)}, bf16[1536,512]{1,0:T(8,128)(2,1)S(1)}, u32[]{:S(2)}) %copy-start.2) | copy-done | bytes 1572888
  27.7 0.8 copy-done.3
  28.5 5.9 %all-to-all-done = bf16[128,8,512]{2,1,0:T(8,128)(2,1)S(1)} async-done(((bf16[128,8,512]{2,1,0:T(8,128)(2,1)}), bf16[128,8,512]{2,1,0:T(8,128)(2,1)S(1)}, u32[]{:S(2)}, u32[]{:S(2)}) %all-to-all-start) | async-done | bytes 1048608 | tf_op jit(solution)/shard_map/all_to_all | solution.py:339
  34.5 1.0 %copy-done.4 = bf16[512,512]{1,0:T(8,128)(2,1)S(1)} copy-done((bf16[512,512]{1,0:T(8,128)(2,1)S(1)}, bf16[512,512]{1,0:T(8,128)(2,1)}, u32[]{:S(2)}) %copy-start.4) | copy-done | bytes 524312
  35.5 13.6 %shard_map.79 = (bf16[1024,256]{1,0:T(8,128)(2,1)}, f32[16,1024]{1,0:T(8,128)S(1)}) custom-call(bf16[1024,512]{1,0:T(8,128)(2,1)S(1)} %bitcast.10, f32[1,512]{1,0:T(1,128)S(1)} %bitcast.11, bf16[512,1536]{1,0:T(8,128)(2,1)S(1)} %copy-done, bf16[1536,512]{1,0:T(8,128)(2,1)} %copy-done.2, bf16[512,512]{1,0:T(8,128)(2,1)S(1)} %copy-done.4, ...), custom_call_target="tpu_custom_call" | custom-call | flops 20000000000 | bytes 8000000 | tf_op jit(solution)/shard_map/pallas_call | solution.py:351
  49.2 0.1 collective-permute-start
  49.3 1.2 %collective-permute-done = f32[8,1024]{1,0:T(8,128)S(1)} collective-permute-done((f32[8,1024]{1,0:T(8,128)S(1)}, f32[8,1024]{1,0:T(8,128)S(1)}, u32[]{:S(2)}, u32[]{:S(2)}) %collective-permute-start) | collective-permute-done | bytes 32800 | tf_op jit(solution)/shard_map/ppermute | solution.py:295
  50.5 0.5 collective-permute-start.2
  51.0 2.1 %collective-permute-start.3 = (f32[8,1024]{1,0:T(8,128)S(1)}, f32[8,1024]{1,0:T(8,128)S(1)}, u32[]{:S(2)}, u32[]{:S(2)}) collective-permute-start(f32[8,1024]{1,0:T(8,128)S(1)} %dynamic-slice_add_fusion), channel_id=1, source_target_pairs={{0,96},{8,104},{2,98},{10,106},{4,100},{12,108},{6,102},{14,110},{... | collective-permute-start | bytes 98312 | tf_op jit(solution)/shard_map/ppermute | solution.py:298
  53.1 1.3 %collective-permute-done.2 = f32[8,1024]{1,0:T(8,128)S(1)} collective-permute-done((f32[8,1024]{1,0:T(8,128)S(1)}, f32[8,1024]{1,0:T(8,128)S(1)}, u32[]{:S(2)}, u32[]{:S(2)}) %collective-permute-start.2) | collective-permute-done | bytes 32800 | tf_op jit(solution)/shard_map/ppermute | solution.py:298
  54.4 0.0 collective-permute-done.3
  54.4 3.0 %collective-permute-done.1 = f32[8,1024]{1,0:T(8,128)S(1)} collective-permute-done((f32[8,1024]{1,0:T(8,128)S(1)}, f32[8,1024]{1,0:T(8,128)S(1)}, u32[]{:S(2)}, u32[]{:S(2)}) %collective-permute-start.1) | collective-permute-done | bytes 32800 | tf_op jit(solution)/shard_map/ppermute | solution.py:298
  57.4 0.3 collective-permute-start.5
  57.7 2.5 %collective-permute-start.6 = (f32[8,1024]{1,0:T(8,128)S(1)}, f32[8,1024]{1,0:T(8,128)S(1)}, u32[]{:S(2)}, u32[]{:S(2)}) collective-permute-start(f32[8,1024]{1,0:T(8,128)S(1)} %add_add_fusion.2), channel_id=1, source_target_pairs={{0,6},{8,14},{2,0},{10,8},{4,2},{12,10},{6,4},{14,12},{16,22},{24,... | collective-permute-start | bytes 98312 | tf_op jit(solution)/shard_map/ppermute | solution.py:298
  60.2 0.0 collective-permute-start.4
  60.2 1.3 %collective-permute-done.5 = f32[8,1024]{1,0:T(8,128)S(1)} collective-permute-done((f32[8,1024]{1,0:T(8,128)S(1)}, f32[8,1024]{1,0:T(8,128)S(1)}, u32[]{:S(2)}, u32[]{:S(2)}) %collective-permute-start.5) | collective-permute-done | bytes 32800 | tf_op jit(solution)/shard_map/ppermute | solution.py:298
  61.5 0.0 collective-permute-done.6
  61.5 3.0 %collective-permute-done.4 = f32[8,1024]{1,0:T(8,128)S(1)} collective-permute-done((f32[8,1024]{1,0:T(8,128)S(1)}, f32[8,1024]{1,0:T(8,128)S(1)}, u32[]{:S(2)}, u32[]{:S(2)}) %collective-permute-start.4) | collective-permute-done | bytes 32800 | tf_op jit(solution)/shard_map/ppermute | solution.py:298
  64.4 0.4 collective-permute-start.8
  64.9 2.3 %collective-permute-start.9 = (f32[8,1024]{1,0:T(8,128)S(1)}, f32[8,1024]{1,0:T(8,128)S(1)}, u32[]{:S(2)}, u32[]{:S(2)}) collective-permute-start(f32[8,1024]{1,0:T(8,128)S(1)} %add_add_fusion.1), channel_id=1, source_target_pairs={{0,17},{8,25},{2,19},{10,27},{4,21},{12,29},{6,23},{14,31},{16,0},... | collective-permute-start | bytes 98312 | tf_op jit(solution)/shard_map/ppermute | solution.py:298
  67.2 0.0 collective-permute-start.7
  67.2 8.5 %all-to-all-start.1 = ((bf16[128,8,256]{2,1,0:T(8,128)(2,1)}), bf16[128,8,256]{2,1,0:T(8,128)(2,1)S(1)}, u32[]{:S(2)}, u32[]{:S(2)}) async-start(bf16[128,8,256]{2,1,0:T(8,128)(2,1)} %bitcast.3), calls=%async_computation.1 | async-start | bytes 1048576 | tf_op jit(solution)/shard_map/all_to_all | solution.py:387
  75.7 0.0 collective-permute-done.9
  75.8 1.1 %collective-permute-start.10 = (f32[8,1024]{1,0:T(8,128)S(1)}, f32[8,1024]{1,0:T(8,128)S(1)}, u32[]{:S(2)}, u32[]{:S(2)}) collective-permute-start(f32[8,1024]{1,0:T(8,128)S(1)} %add_add_fusion), channel_id=1, source_target_pairs={{0,8},{1,9},{2,10},{3,11},{4,12},{5,13},{6,14},{7,15},{8,0},{9,1},... | collective-permute-start | bytes 98312 | tf_op jit(solution)/shard_map/ppermute | solution.py:300
  76.9 0.9 collective-permute-done.10
  77.8 0.1 reshape.38
  78.0 0.1 reshape.39
  78.1 0.2 fusion
  78.3 0.8 copy.15
  79.2 10.6 %all-to-all-done.1 = bf16[128,8,256]{2,1,0:T(8,128)(2,1)S(1)} async-done(((bf16[128,8,256]{2,1,0:T(8,128)(2,1)}), bf16[128,8,256]{2,1,0:T(8,128)(2,1)S(1)}, u32[]{:S(2)}, u32[]{:S(2)}) %all-to-all-start.1) | async-done | bytes 524320 | tf_op jit(solution)/shard_map/all_to_all | solution.py:387
  89.8 1.1 %shard_map.80 = bf16[16,32,512]{2,1,0:T(8,128)(2,1)} custom-call(bf16[1024,256]{1,0:T(8,128)(2,1)S(1)} %bitcast.9), custom_call_target="tpu_custom_call" | custom-call | tf_op jit(solution)/shard_map/pallas_call | solution.py:391
  (18 shorter events, 0.1 us)
Async XLA Ops:
  3.3 11.5 %copy-start.6 = (f32[16,31,31]{2,0,1:T(8,128)S(1)}, f32[16,31,31]{2,0,1:T(8,128)}, u32[]{:S(2)}) copy-start(f32[16,31,31]{2,0,1:T(8,128)} %param.11) | copy-start | bytes 184516
  3.4 31.1 %all-to-all-start = ((bf16[128,8,512]{2,1,0:T(8,128)(2,1)}), bf16[128,8,512]{2,1,0:T(8,128)(2,1)S(1)}, u32[]{:S(2)}, u32[]{:S(2)}) async-start(bf16[128,8,512]{2,1,0:T(8,128)(2,1)} %bitcast.12), calls=%async_computation | async-start | bytes 2097152 | tf_op jit(solution)/shard_map/all_to_all | solution.py:339
  15.1 1.0 %copy-start.1 = (bf16[512,512]{1,0:T(8,128)(2,1)S(1)}, bf16[512,512]{1,0:T(8,128)(2,1)}, u32[]{:S(2)}) copy-start(bf16[512,512]{1,0:T(8,128)(2,1)} %wout_ref.1) | copy-start | bytes 1572868
  15.7 18.8 %copy-start = (bf16[512,1536]{1,0:T(8,128)(2,1)S(1)}, bf16[512,1536]{1,0:T(8,128)(2,1)}, u32[]{:S(2)}) copy-start(bf16[512,1536]{1,0:T(8,128)(2,1)} %win_ref.3) | copy-start | bytes 4718596
  15.7 18.7 %copy-start.5 = (f32[512]{0:T(512)S(1)}, f32[512]{0:T(512)}, u32[]{:S(2)}) copy-start(f32[512]{0:T(512)} %param.8) | copy-start | bytes 6148
  26.5 1.2 %copy-start.2 = (bf16[1536,512]{1,0:T(8,128)(2,1)}, bf16[1536,512]{1,0:T(8,128)(2,1)S(1)}, u32[]{:S(2)}) copy-start(bf16[1536,512]{1,0:T(8,128)(2,1)S(1)} %get-tuple-element.7.win_t_hbm) | copy-start | bytes 4718596
  27.7 0.8 copy-start.3
  34.4 1.0 %copy-start.4 = (bf16[512,512]{1,0:T(8,128)(2,1)S(1)}, bf16[512,512]{1,0:T(8,128)(2,1)}, u32[]{:S(2)}) copy-start(bf16[512,512]{1,0:T(8,128)(2,1)} %copy-done.3) | copy-start | bytes 1572868
  49.2 1.3 %collective-permute-start = (f32[8,1024]{1,0:T(8,128)S(1)}, f32[8,1024]{1,0:T(8,128)S(1)}, u32[]{:S(2)}, u32[]{:S(2)}) collective-permute-start(f32[8,1024]{1,0:T(8,128)S(1)} %constant_dynamic-slice_fusion), channel_id=1, source_target_pairs={{0,8},{1,9},{2,10},{3,11},{4,12},{5,13},{6,14},{7,15},{8,0},{9,1},... | collective-permute-start | bytes 98312 | tf_op jit(solution)/shard_map/ppermute | solution.py:295
  50.5 4.0 %collective-permute-start.2 = (f32[8,1024]{1,0:T(8,128)S(1)}, f32[8,1024]{1,0:T(8,128)S(1)}, u32[]{:S(2)}, u32[]{:S(2)}) collective-permute-start(f32[8,1024]{1,0:T(8,128)S(1)} %dynamic-slice_add_fusion), channel_id=1, source_target_pairs={{0,32},{8,40},{2,34},{10,42},{4,36},{12,44},{6,38},{14,46},{16,48}... | collective-permute-start | bytes 98312 | tf_op jit(solution)/shard_map/ppermute | solution.py:298
  51.0 3.4 %collective-permute-start.3 = (f32[8,1024]{1,0:T(8,128)S(1)}, f32[8,1024]{1,0:T(8,128)S(1)}, u32[]{:S(2)}, u32[]{:S(2)}) collective-permute-start(f32[8,1024]{1,0:T(8,128)S(1)} %dynamic-slice_add_fusion), channel_id=1, source_target_pairs={{0,96},{8,104},{2,98},{10,106},{4,100},{12,108},{6,102},{14,110},{... | collective-permute-start | bytes 98312 | tf_op jit(solution)/shard_map/ppermute | solution.py:298
  53.1 4.3 %collective-permute-start.1 = (f32[8,1024]{1,0:T(8,128)S(1)}, f32[8,1024]{1,0:T(8,128)S(1)}, u32[]{:S(2)}, u32[]{:S(2)}) collective-permute-start(f32[8,1024]{1,0:T(8,128)S(1)} %dynamic-slice_add_fusion), channel_id=1, source_target_pairs={{0,64},{8,72},{2,66},{10,74},{4,68},{12,76},{6,70},{14,78},{16,80}... | collective-permute-start | bytes 98312 | tf_op jit(solution)/shard_map/ppermute | solution.py:298
  57.4 4.0 %collective-permute-start.5 = (f32[8,1024]{1,0:T(8,128)S(1)}, f32[8,1024]{1,0:T(8,128)S(1)}, u32[]{:S(2)}, u32[]{:S(2)}) collective-permute-start(f32[8,1024]{1,0:T(8,128)S(1)} %add_add_fusion.2), channel_id=1, source_target_pairs={{0,2},{8,10},{2,4},{10,12},{4,6},{12,14},{6,0},{14,8},{16,18},{24,... | collective-permute-start | bytes 98312 | tf_op jit(solution)/shard_map/ppermute | solution.py:298
  57.7 3.8 %collective-permute-start.6 = (f32[8,1024]{1,0:T(8,128)S(1)}, f32[8,1024]{1,0:T(8,128)S(1)}, u32[]{:S(2)}, u32[]{:S(2)}) collective-permute-start(f32[8,1024]{1,0:T(8,128)S(1)} %add_add_fusion.2), channel_id=1, source_target_pairs={{0,6},{8,14},{2,0},{10,8},{4,2},{12,10},{6,4},{14,12},{16,22},{24,... | collective-permute-start | bytes 98312 | tf_op jit(solution)/shard_map/ppermute | solution.py:298
  60.2 4.3 %collective-permute-start.4 = (f32[8,1024]{1,0:T(8,128)S(1)}, f32[8,1024]{1,0:T(8,128)S(1)}, u32[]{:S(2)}, u32[]{:S(2)}) collective-permute-start(f32[8,1024]{1,0:T(8,128)S(1)} %add_add_fusion.2), channel_id=1, source_target_pairs={{0,4},{8,12},{2,6},{10,14},{4,0},{12,8},{6,2},{14,10},{16,20},{24,... | collective-permute-start | bytes 98312 | tf_op jit(solution)/shard_map/ppermute | solution.py:298
  64.4 11.3 %collective-permute-start.8 = (f32[8,1024]{1,0:T(8,128)S(1)}, f32[8,1024]{1,0:T(8,128)S(1)}, u32[]{:S(2)}, u32[]{:S(2)}) collective-permute-start(f32[8,1024]{1,0:T(8,128)S(1)} %add_add_fusion.1), channel_id=1, source_target_pairs={{0,16},{8,24},{2,18},{10,26},{4,20},{12,28},{6,22},{14,30},{16,1},... | collective-permute-start | bytes 98312 | tf_op jit(solution)/shard_map/ppermute | solution.py:298
  64.9 10.9 %collective-permute-start.9 = (f32[8,1024]{1,0:T(8,128)S(1)}, f32[8,1024]{1,0:T(8,128)S(1)}, u32[]{:S(2)}, u32[]{:S(2)}) collective-permute-start(f32[8,1024]{1,0:T(8,128)S(1)} %add_add_fusion.1), channel_id=1, source_target_pairs={{0,17},{8,25},{2,19},{10,27},{4,21},{12,29},{6,23},{14,31},{16,0},... | collective-permute-start | bytes 98312 | tf_op jit(solution)/shard_map/ppermute | solution.py:298
  67.2 8.6 %collective-permute-start.7 = (f32[8,1024]{1,0:T(8,128)S(1)}, f32[8,1024]{1,0:T(8,128)S(1)}, u32[]{:S(2)}, u32[]{:S(2)}) collective-permute-start(f32[8,1024]{1,0:T(8,128)S(1)} %add_add_fusion.1), channel_id=1, source_target_pairs={{0,1},{8,9},{2,3},{10,11},{4,5},{12,13},{6,7},{14,15},{16,17},{24,... | collective-permute-start | bytes 98312 | tf_op jit(solution)/shard_map/ppermute | solution.py:298
  67.2 22.6 %all-to-all-start.1 = ((bf16[128,8,256]{2,1,0:T(8,128)(2,1)}), bf16[128,8,256]{2,1,0:T(8,128)(2,1)S(1)}, u32[]{:S(2)}, u32[]{:S(2)}) async-start(bf16[128,8,256]{2,1,0:T(8,128)(2,1)} %bitcast.3), calls=%async_computation.1 | async-start | bytes 1048576 | tf_op jit(solution)/shard_map/all_to_all | solution.py:387
  75.8 2.0 %collective-permute-start.10 = (f32[8,1024]{1,0:T(8,128)S(1)}, f32[8,1024]{1,0:T(8,128)S(1)}, u32[]{:S(2)}, u32[]{:S(2)}) collective-permute-start(f32[8,1024]{1,0:T(8,128)S(1)} %add_add_fusion), channel_id=1, source_target_pairs={{0,8},{1,9},{2,10},{3,11},{4,12},{5,13},{6,14},{7,15},{8,0},{9,1},... | collective-permute-start | bytes 98312 | tf_op jit(solution)/shard_map/ppermute | solution.py:300

commit v3 on v2

--- a/solution.py
+++ b/solution.py
@@ -14,6 +14,7 @@
 F32 = jnp.float32
 SMALL_GRANT = 12 << 20
 LARGE_GRANT = 50 << 20
+LINE_ROWS = 2048
 
 
 def iota(shape, dim):
@@ -82,7 +83,7 @@
     return jnp.dot(a, b, preferred_element_type=F32)
 
 
-def prep_kernel(near_ref, far_ref, win_ref, wout_ref, bias_ref, win_t_ref, wout_t_ref):
+def prep_kernel(near_ref, far_ref, win_ref, wout_ref, line_hbm, turned_ref, line_ref, sem):
     row = iota((16, 512), 0)
     ahead = (bits(iota((16, 512), 1), 0, 4) + row) < 16
 
@@ -90,37 +91,39 @@
         line = jnp.where(ahead, near_ref[pl.ds(h, 1), :], far_ref[pl.ds(h, 1), :])
         for b in (1, 2, 4, 8):
             line = jnp.where(lax.bitwise_and(row, b) != 0, pltpu.roll(line, b, 1), line)
-        for r in range(8):
-            turned = line if r == 0 else pltpu.roll(line, 512 - 16 * r, 1)
-            bias_ref[h, 16 * (15 - r) : 16 * (15 - r) + 16, :] = turned[:, 0:256]
-            bias_ref[h, 16 * (7 - r) : 16 * (7 - r) + 16, :] = turned[:, 128:384]
+        line_ref[pl.ds(pl.multiple_of(16 * h, 16), 16), :] = line
         return carry
 
     lax.fori_loop(0, HEADS, head, 0)
+    emit = pltpu.make_async_copy(line_ref, line_hbm.at[pl.ds(0, 256)], sem)
+    emit.start()
     for part in range(3):
         cols = slice(D * part, D * part + D)
-        win_t_ref[cols, :] = win_ref[:, cols].astype(F32).T.astype(BF16)
-    wout_t_ref[...] = wout_ref[...].astype(F32).T.astype(BF16)
+        turned_ref[cols, :] = win_ref[:, cols].astype(F32).T.astype(BF16)
+    turned_ref[3 * D : 4 * D, :] = wout_ref[...].astype(F32).T.astype(BF16)
+    emit.wait()
 
 
 def group_kernel(
-    recv_ref, gain_ref, win_ref, win_t_hbm, wout_t_hbm, bias_hbm,
+    recv_ref, gain_ref, win_ref, line_hbm, turned_hbm,
     out_ref, pn_ref,
     unit_ref, inv_ref, q_ref, k_ref, v_ref, go_ref, qt_ref, kt_ref, got_ref,
     dqt_ref, dk_ref, dv_ref, tok_ref, cot_ref, dk_part, dv_part,
-    win_t_ref, wout_t_ref, bias_ref, weight_sem, bias_sem,
+    win_t_ref, wout_t_ref, bias_ref, line_ref, weight_sem,
 ):
     scale = HEAD_DIM ** (-0.5)
-    fetch_out = pltpu.make_async_copy(wout_t_hbm, wout_t_ref, weight_sem.at[0])
-    fetch_in = pltpu.make_async_copy(win_t_hbm, win_t_ref, weight_sem.at[1])
-
-    def fetch_bias(hb):
-        four = pl.ds(4 * hb, 4)
-        return pltpu.make_async_copy(bias_hbm.at[four], bias_ref.at[four], bias_sem.at[hb])
-
+    fetch_out = pltpu.make_async_copy(
+        turned_hbm.at[pl.ds(3 * D, D)], wout_t_ref, weight_sem.at[0]
+    )
+    fetch_in = pltpu.make_async_copy(
+        turned_hbm.at[pl.ds(0, 3 * D)], win_t_ref, weight_sem.at[1]
+    )
+
+    fetch_lines = pltpu.make_async_copy(
+        line_hbm.at[pl.ds(0, 256)], line_ref, weight_sem.at[2]
+    )
     fetch_out.start()
-    for hb in range(4):
-        fetch_bias(hb).start()
+    fetch_lines.start()
     fetch_in.start()
     take = one_hot(
         lambda o: bits(o, 1, 5) * 8 + bits(o, 7, 1) * 4 + bits(o, 6, 1) * 2 + bits(o, 0, 1)
@@ -167,7 +170,6 @@
 
     def block(hb, carry):
         lanes = pl.ds(pl.multiple_of(hb * 128, 128), 128)
-        fetch_bias(hb).wait()
 
         def thin(g, hh):
             return pl.ds(pl.multiple_of(D * g + hb * 128 + 32 * hh, 32), 32)
@@ -178,37 +180,25 @@
             grad_probs = dot_nn(v_ref[sl, lanes], only(got_ref[thin(g, hh), :], hh))
             return scores, grad_probs
 
-        def backward(hh, g, scores, grad_probs):
+        def soft(hh, scores, grad_probs, t):
+            shifted = scores[:, t] + bias_ref[hh, :, t]
+            exponent = jnp.exp(shifted - jnp.max(shifted, axis=0, keepdims=True))
+            probs = exponent * (1.0 / jnp.sum(exponent, axis=0, keepdims=True))
+            delta = jnp.sum(probs * grad_probs[:, t], axis=0, keepdims=True)
+            grad = probs * (grad_probs[:, t] - delta)
+            return probs.astype(BF16), grad.astype(BF16), grad
+
+        def weigh_values(hh, g, probs_half):
             sl = slice(256 * g, 256 * g + 256)
-            probs_half, scores_half, grads = [], [], []
-            for t in (slice(0, 128), slice(128, 256)):
-                shifted = scores[:, t] + bias_ref[hb * 4 + hh, :, t]
-                exponent = jnp.exp(shifted - jnp.max(shifted, axis=0, keepdims=True))
-                probs = exponent * (1.0 / jnp.sum(exponent, axis=0, keepdims=True))
-                probs_half.append(probs.astype(BF16))
-                delta = jnp.sum(probs * grad_probs[:, t], axis=0, keepdims=True)
-                grad = probs * (grad_probs[:, t] - delta)
-                scores_half.append(grad.astype(BF16))
-                grads.append(grad)
-            half = jnp.concatenate(scores_half, axis=1)
-            mine = owner == hh
-            grad_v = dot_nn(jnp.concatenate(probs_half, axis=1), go_ref[sl, lanes])
-            pltpu.store(dv_part.at[sl, :], grad_v, mask=mine)
-            pltpu.store(dk_part.at[sl, :], dot_nn(half, q_ref[sl, lanes]), mask=mine)
+            grad_v = dot_nn(probs_half, go_ref[sl, lanes])
+            pltpu.store(dv_part.at[sl, :], grad_v, mask=owner == hh)
+
+        def weigh_scores(hh, g, half):
+            sl = slice(256 * g, 256 * g + 256)
+            pltpu.store(dk_part.at[sl, :], dot_nn(half, q_ref[sl, lanes]), mask=owner == hh)
             dqt_ref[thin(g, hh), :] = dot_nn(kt_ref[thin(g, hh), :], half) * scale
-            return grads
-
-        units = [(hh, g) for hh in range(4) for g in range(2)]
-        ready = forward(*units[0])
-        total = None
-        for n, (hh, g) in enumerate(units):
-            after = forward(*units[n + 1]) if n + 1 < len(units) else None
-            grads = backward(hh, g, *ready)
-            ready = after
-            if g == 0:
-                total = grads
-                continue
-            left, right = total[0] + grads[0], total[1] + grads[1]
+
+        def fold_table(hh, left, right):
             fold = None
             blank = jnp.zeros((16, 128), F32)
             for r in range(8):
@@ -224,10 +214,46 @@
             h = hb * 4 + hh
             pn_ref[pl.ds(h, 1), 0:512] = jnp.sum(near, axis=0, keepdims=True)
             pn_ref[pl.ds(h, 1), 512:1024] = jnp.sum(fold - near, axis=0, keepdims=True)
+
+        def spread_bias(hh):
+            line = line_ref[pl.ds(pl.multiple_of(64 * hb + 16 * hh, 16), 16), :]
+            for r in range(8):
+                turned = line if r == 0 else pltpu.roll(line, 512 - 16 * r, 1)
+                bias_ref[hh, 16 * (15 - r) : 16 * (15 - r) + 16, :] = turned[:, 0:256]
+                bias_ref[hh, 16 * (7 - r) : 16 * (7 - r) + 16, :] = turned[:, 128:384]
+
+        units = [(hh, g) for hh in range(4) for g in range(2)]
+        spread_bias(0)
+        ready = forward(*units[0])
+        total = late = None
+        for n, (hh, g) in enumerate(units):
+            after = forward(*units[n + 1]) if n + 1 < len(units) else None
+            low = soft(hh, *ready, slice(0, 128))
+            if late is not None:
+                weigh_values(*late[0:3])
+            if g == 0 and hh < 3:
+                spread_bias(hh + 1)
+            high = soft(hh, *ready, slice(128, 256))
+            if late is not None:
+                weigh_scores(*late[0:2], late[3])
+            ready = after
+            late = (
+                hh,
+                g,
+                jnp.concatenate([low[0], high[0]], axis=1),
+                jnp.concatenate([low[1], high[1]], axis=1),
+            )
+            if g == 0:
+                total = low[2], high[2]
+            else:
+                fold_table(hh, total[0] + low[2], total[1] + high[2])
+        weigh_values(*late[0:3])
+        weigh_scores(*late[0:2], late[3])
         dk_ref[:, lanes] = dk_part[...].astype(BF16)
         dv_ref[:, lanes] = dv_part[...].astype(BF16)
         return carry
 
+    fetch_lines.wait()
     lax.fori_loop(0, 4, block, 0)
     fetch_in.wait()
 
@@ -267,18 +293,19 @@
     return (z * 4 + (y % 2) * 2 + core) * 8 + x * 2 + y // 2
 
 
-def shift_pairs(axis, step):
+def shift_pairs(turn, step):
     pairs = []
     for z in range(4):
         for y in range(4):
             for x in range(4):
                 for core in range(2):
-                    there = {"z": z, "y": y, "x": x}
-                    there[axis] = (there[axis] + step) % 4
+                    there = [z, x, y]
+                    along = (turn + core) % 3
+                    there[along] = (there[along] + step) % 4
                     pairs.append(
                         (
                             device_index(z, y, x, core),
-                            device_index(there["z"], there["y"], there["x"], core),
+                            device_index(there[0], there[2], there[1], core),
                         )
                     )
     return pairs
@@ -294,8 +321,8 @@
     given = lax.dynamic_slice(part, (8 * (1 - core), 0), (8, 1024))
     got = lax.ppermute(given, AXES, other_core_pairs())
     own = own + got
-    for axis in ("z", "x", "y"):
-        one, two, three = (lax.ppermute(own, AXES, shift_pairs(axis, s)) for s in (1, 2, 3))
+    for turn in range(3):
+        one, two, three = (lax.ppermute(own, AXES, shift_pairs(turn, s)) for s in (1, 2, 3))
         own = (own + two) + (one + three)
     other = lax.ppermute(own, AXES, other_core_pairs())
     low = jnp.where(core == 0, own, other)
@@ -312,10 +339,10 @@
 
 
 def join_table(part):
-    near = part[:, 0:512].reshape(HEADS, 32, 16)[:, 0:31]
-    far = part[:, 512:1024].reshape(HEADS, 32, 16)
-    far = jnp.concatenate([far[:, 31:32], far[:, 0:30]], axis=1)[:, :, 1:16]
-    return jnp.concatenate([far, near], axis=2)
+    by_row = part.reshape(HEADS, 2, 32, 16).transpose(2, 0, 1, 3)
+    near = by_row[0:31, :, 0]
+    far = jnp.concatenate([by_row[31:32, :, 1], by_row[0:30, :, 1]], axis=0)[:, :, 1:16]
+    return jnp.concatenate([far, near], axis=2).transpose(1, 0, 2)
 
 
 def vmem_specs(count):
@@ -337,15 +364,15 @@
     )(tokens, cotangent)
     near, far = split_bias(bias_table)
     got = lax.all_to_all(sent.reshape(128, 8, D), AXES, split_axis=0, concat_axis=0, tiled=True)
-    bias, in_turned, out_turned = pl.pallas_call(
+    lines, turned = pl.pallas_call(
         prep_kernel,
         out_shape=(
-            jax.ShapeDtypeStruct((HEADS, 256, 256), F32),
-            jax.ShapeDtypeStruct((3 * D, D), BF16),
-            jax.ShapeDtypeStruct((D, D), BF16),
+            jax.ShapeDtypeStruct((LINE_ROWS, 512), F32),
+            jax.ShapeDtypeStruct((4 * D, D), BF16),
         ),
         in_specs=vmem_specs(4),
-        out_specs=tuple(vmem_specs(3)),
+        out_specs=(pl.BlockSpec(memory_space=pl.ANY), vmem_specs(1)[0]),
+        scratch_shapes=[pltpu.VMEM((256, 512), F32), pltpu.SemaphoreType.DMA],
         compiler_params=pltpu.CompilerParams(vmem_limit_bytes=LARGE_GRANT),
     )(near, far, in_weight, out_weight)
     back, part = pl.pallas_call(
@@ -354,7 +381,7 @@
             jax.ShapeDtypeStruct((1024, 256), BF16),
             jax.ShapeDtypeStruct((HEADS, 1024), F32),
         ),
-        in_specs=vmem_specs(3) + [pl.BlockSpec(memory_space=pltpu.HBM)] * 3,
+        in_specs=vmem_specs(3) + [pl.BlockSpec(memory_space=pltpu.HBM)] * 2,
         out_specs=tuple(vmem_specs(2)),
         scratch_shapes=[
             pltpu.VMEM((512, D), F32),
@@ -375,26 +402,27 @@
             pltpu.VMEM((512, 128), F32),
             pltpu.VMEM((3 * D, D), BF16),
             pltpu.VMEM((D, D), BF16),
-            pltpu.VMEM((HEADS, 256, 256), F32),
-            pltpu.SemaphoreType.DMA((2,)),
-            pltpu.SemaphoreType.DMA((4,)),
+            pltpu.VMEM((4, 256, 256), F32),
+            pltpu.VMEM((256, 512), F32),
+            pltpu.SemaphoreType.DMA((3,)),
         ],
         compiler_params=pltpu.CompilerParams(vmem_limit_bytes=LARGE_GRANT),
         cost_estimate=pl.CostEstimate(
             flops=20_000_000_000, bytes_accessed=8_000_000, transcendentals=2_000_000
         ),
-    )(got.reshape(1024, D), norm_gain.reshape(1, D), in_weight, in_turned, out_turned, bias)
+    )(got.reshape(1024, D), norm_gain.reshape(1, D), in_weight, lines, turned)
     returned = lax.all_to_all(
         back.reshape(128, 8, 256), AXES, split_axis=0, concat_axis=0, tiled=True
     )
     table = join_table(sum_everywhere(part))
-    grad_input = pl.pallas_call(
+    unpack = pl.pallas_call(
         unpack_kernel,
         out_shape=jax.ShapeDtypeStruct((16, 32, D), BF16),
         in_specs=vmem_specs(1),
         out_specs=vmem_specs(1)[0],
         compiler_params=pltpu.CompilerParams(vmem_limit_bytes=SMALL_GRANT),
-    )(returned.reshape(1024, 256))
+    )
+    grad_input = unpack(returned.reshape(1024, 256))
     return (grad_input, table)
 
 

time: 91.2 us -> 94.6 us (1.037)
  waiting for transfers between devices: 27.1 us -> 36.3 us
  Pallas kernels: 27.8 us -> 24.5 us
  local copies, waits for them, and re-layouts: 5.22 us -> 3.69 us
    all_to_all x1, starting transfers between devices: 8.53 us -> 3.55 us  [step(): lax.all_to_all(back.reshape(128, 8, 256), AXES, split_axis=0, concat_axis...]
    ppermute x9, waiting for transfers between devices: 8.53 us -> 12.8 us  [sum_everywhere(): lax.ppermute(own, AXES, shift_pairs(turn, s))]
    ppermute x1, starting transfers between devices: 1.15 us -> 5.37 us  [sum_everywhere(): other = lax.ppermute(own, AXES, other_core_pairs())]
    all_to_all x1, waiting for transfers between devices: 5.94 us -> 9.6 us  [step(): lax.all_to_all(sent.reshape(128, 8, D), AXES, split_axis=0, concat_axis=0...]
    unnamed x16 -> x10, local copies, waits for them, and re-layouts: 4.15 us -> 0.96 us
    pallas_call x2, Pallas kernels: 11.5 us -> 8.32 us  [the longest x1 7.21 us: step(): pl.pallas_call(prep_kernel, out_shape=(jax.ShapeDtypeStruct((LINE_ROWS, 5...]
    all_to_all x1, waiting for transfers between devices: 10.6 us -> 12.7 us  [step(): lax.all_to_all(back.reshape(128, 8, 256), AXES, split_axis=0, concat_axis...]
    reshape x2, local copies, waits for them, and re-layouts: 0.31 us -> 1.26 us  [split_bias(): return (near.reshape(HEADS, 512), far.reshape(HEADS, 512))]
  transfers between devices with their start and end apart: 13 -> 13, of which waited for: 8 -> 9; matrix products, arithmetic and copies ran while one was open for 3% -> 4% of each run, Pallas kernels for 11% -> 8%
where the time goes in v3:
time: 94.6 us; the launch traced here: 94.4 us
  waiting for transfers between devices  36.3 us (38%)
  starting transfers between devices  28.7 us (30%)
  Pallas kernels  24.5 us (26%)
  local copies, waits for them, and re-layouts  3.69 us (4%)
    pallas_call x1, Pallas kernels, step(): pl.pallas_call(group_kernel, out_shape=(jax.ShapeDtypeStruct((1024, 256),...  13.4 us
    ppermute x9, waiting for transfers between devices, sum_everywhere(): lax.ppermute(own, AXES, shift_pairs(turn, s))  12.8 us
    all_to_all x1, waiting for transfers between devices, step(): lax.all_to_all(back.reshape(128, 8, 256), AXES, split_axis=0, concat_axis...  12.7 us
    all_to_all x1, starting transfers between devices, step(): lax.all_to_all(sent.reshape(128, 8, D), AXES, split_axis=0, concat_axis=0...  11.5 us
    all_to_all x1, waiting for transfers between devices, step(): lax.all_to_all(sent.reshape(128, 8, D), AXES, split_axis=0, concat_axis=0...  9.6 us
    ppermute x9, starting transfers between devices, sum_everywhere(): lax.ppermute(own, AXES, shift_pairs(turn, s))  8.17 us
    pallas_call x1, Pallas kernels, step(): pl.pallas_call(prep_kernel, out_shape=(jax.ShapeDtypeStruct((LINE_ROWS, 5...  7.21 us
    ppermute x1, starting transfers between devices, sum_everywhere(): other = lax.ppermute(own, AXES, other_core_pairs())  5.37 us
  transfers between devices with their start and end apart: 13, of which 9 were waited for; matrix products, arithmetic and copies ran while one was open for 4% of the time, Pallas kernels for 8%

profile of v3, /device:TPU:1, one launch (start us, length us, event | category | flops | bytes accessed | tf_op | source)
XLA Modules:
  0.0 94.4 jit_solution(12953585427777142397)
XLA Ops:
  0.6 0.0 copy-start.3
  0.6 2.7 %shard_map.77 = bf16[1024,512]{1,0:T(8,128)(2,1)} custom-call(bf16[16,32,512]{2,1,0:T(8,128)(2,1)} %tok_hbm.1, bf16[16,32,512]{2,1,0:T(8,128)(2,1)} %cot_hbm.1), custom_call_target="tpu_custom_call" | custom-call | tf_op jit(solution)/shard_map/pallas_call | solution.py:353
  3.4 11.5 %all-to-all-start = ((bf16[128,8,512]{2,1,0:T(8,128)(2,1)}), bf16[128,8,512]{2,1,0:T(8,128)(2,1)S(1)}, u32[]{:S(2)}, u32[]{:S(2)}) async-start(bf16[128,8,512]{2,1,0:T(8,128)(2,1)} %bitcast.23), calls=%async_computation | async-start | bytes 2097152 | tf_op jit(solution)/shard_map/all_to_all | solution.py:366
  14.9 0.0 copy-start
  14.9 0.0 copy-start.1
  14.9 0.0 copy-done.3
  14.9 0.1 slice.24
  15.0 0.1 copy.19
  15.1 0.7 concatenate.15.clone
  15.9 1.1 %reshape.31.near_ref = f32[16,512]{1,0:T(8,128)S(1)} reshape(f32[16,32,16]{2,1,0:T(8,128)} %concatenate.15.clone) | data formatting | bytes 65536 | tf_op jit(solution)/shard_map/reshape | solution.py:338
  17.0 0.1 pad.13.clone
  17.1 0.1 pad_slice_fusion
  17.1 0.1 pad_slice_fusion.1
  17.3 0.1 pad_maximum_fusion.1
  17.4 0.1 copy.13
  17.5 0.2 reshape.32.far_ref
  17.6 0.0 copy-done
  17.6 7.2 %shard_map.78 = (f32[2048,512]{1,0:T(8,128)}, bf16[2048,512]{1,0:T(8,128)(2,1)}) custom-call(f32[16,512]{1,0:T(8,128)S(1)} %reshape.31.near_ref, f32[16,512]{1,0:T(8,128)S(1)} %reshape.32.far_ref, bf16[512,1536]{1,0:T(8,128)(2,1)S(1)} %copy-done, bf16[512,512]{1,0:T(8,128)(2,1)S(1)} %copy-done.1), custom_call_target="tpu_custom_call" | custom-call | tf_op jit(solution)/shard_map/pallas_call | solution.py:367
  24.9 9.6 %all-to-all-done = bf16[128,8,512]{2,1,0:T(8,128)(2,1)S(1)} async-done(((bf16[128,8,512]{2,1,0:T(8,128)(2,1)}), bf16[128,8,512]{2,1,0:T(8,128)(2,1)S(1)}, u32[]{:S(2)}, u32[]{:S(2)}) %all-to-all-start) | async-done | bytes 1048608 | tf_op jit(solution)/shard_map/all_to_all | solution.py:366
  34.5 13.4 %shard_map.79 = (bf16[1024,256]{1,0:T(8,128)(2,1)}, f32[16,1024]{1,0:T(8,128)S(1)}) custom-call(bf16[1024,512]{1,0:T(8,128)(2,1)S(1)} %bitcast.21, f32[1,512]{1,0:T(1,128)S(1)} %bitcast.22, bf16[512,1536]{1,0:T(8,128)(2,1)S(1)} %copy-done, f32[2048,512]{1,0:T(8,128)} %get-tuple-element.6.line_hbm, bf16[2048,512]{1,0:T(8,128)(2,1)} %get-tuple-element.7.turned_hbm), custom_call_target="tpu_custom_call" | custom-call | flops 20000000000 | bytes 8000000 | tf_op jit(solution)/shard_map/pallas_call | solution.py:378
  47.9 0.1 collective-permute-start
  48.0 1.2 %collective-permute-done = f32[8,1024]{1,0:T(8,128)S(1)} collective-permute-done((f32[8,1024]{1,0:T(8,128)S(1)}, f32[8,1024]{1,0:T(8,128)S(1)}, u32[]{:S(2)}, u32[]{:S(2)}) %collective-permute-start) | collective-permute-done | bytes 32800 | tf_op jit(solution)/shard_map/ppermute | solution.py:322
  49.2 0.2 collective-permute-start.2
  49.4 2.5 %collective-permute-start.3 = (f32[8,1024]{1,0:T(8,128)S(1)}, f32[8,1024]{1,0:T(8,128)S(1)}, u32[]{:S(2)}, u32[]{:S(2)}) collective-permute-start(f32[8,1024]{1,0:T(8,128)S(1)} %dynamic-slice_add_fusion), channel_id=1, source_target_pairs={{0,96},{8,14},{2,98},{10,8},{4,100},{12,10},{6,102},{14,12},{16,11... | collective-permute-start | bytes 98312 | tf_op jit(solution)/shard_map/ppermute | solution.py:325
  51.9 0.0 collective-permute-start.1
  51.9 1.3 %collective-permute-done.2 = f32[8,1024]{1,0:T(8,128)S(1)} collective-permute-done((f32[8,1024]{1,0:T(8,128)S(1)}, f32[8,1024]{1,0:T(8,128)S(1)}, u32[]{:S(2)}, u32[]{:S(2)}) %collective-permute-start.2) | collective-permute-done | bytes 32800 | tf_op jit(solution)/shard_map/ppermute | solution.py:325
  53.2 0.0 collective-permute-done.3
  53.2 3.0 %collective-permute-done.1 = f32[8,1024]{1,0:T(8,128)S(1)} collective-permute-done((f32[8,1024]{1,0:T(8,128)S(1)}, f32[8,1024]{1,0:T(8,128)S(1)}, u32[]{:S(2)}, u32[]{:S(2)}) %collective-permute-start.1) | collective-permute-done | bytes 32800 | tf_op jit(solution)/shard_map/ppermute | solution.py:325
  56.2 0.4 collective-permute-start.5
  56.6 2.3 %collective-permute-start.6 = (f32[8,1024]{1,0:T(8,128)S(1)}, f32[8,1024]{1,0:T(8,128)S(1)}, u32[]{:S(2)}, u32[]{:S(2)}) collective-permute-start(f32[8,1024]{1,0:T(8,128)S(1)} %add_add_fusion.2), channel_id=1, source_target_pairs={{0,6},{8,25},{2,0},{10,27},{4,2},{12,29},{6,4},{14,31},{16,22},{24... | collective-permute-start | bytes 98312 | tf_op jit(solution)/shard_map/ppermute | solution.py:325
  58.9 0.0 collective-permute-start.4
  58.9 1.3 %collective-permute-done.5 = f32[8,1024]{1,0:T(8,128)S(1)} collective-permute-done((f32[8,1024]{1,0:T(8,128)S(1)}, f32[8,1024]{1,0:T(8,128)S(1)}, u32[]{:S(2)}, u32[]{:S(2)}) %collective-permute-start.5) | collective-permute-done | bytes 32800 | tf_op jit(solution)/shard_map/ppermute | solution.py:325
  60.2 0.0 collective-permute-done.6
  60.2 3.0 %collective-permute-done.4 = f32[8,1024]{1,0:T(8,128)S(1)} collective-permute-done((f32[8,1024]{1,0:T(8,128)S(1)}, f32[8,1024]{1,0:T(8,128)S(1)}, u32[]{:S(2)}, u32[]{:S(2)}) %collective-permute-start.4) | collective-permute-done | bytes 32800 | tf_op jit(solution)/shard_map/ppermute | solution.py:325
  63.2 0.6 collective-permute-start.8
  63.8 2.1 %collective-permute-start.9 = (f32[8,1024]{1,0:T(8,128)S(1)}, f32[8,1024]{1,0:T(8,128)S(1)}, u32[]{:S(2)}, u32[]{:S(2)}) collective-permute-start(f32[8,1024]{1,0:T(8,128)S(1)} %add_add_fusion.1), channel_id=1, source_target_pairs={{0,17},{8,104},{2,19},{10,106},{4,21},{12,108},{6,23},{14,110},{16... | collective-permute-start | bytes 98312 | tf_op jit(solution)/shard_map/ppermute | solution.py:325
  66.0 0.0 collective-permute-start.7
  66.0 1.3 %collective-permute-done.8 = f32[8,1024]{1,0:T(8,128)S(1)} collective-permute-done((f32[8,1024]{1,0:T(8,128)S(1)}, f32[8,1024]{1,0:T(8,128)S(1)}, u32[]{:S(2)}, u32[]{:S(2)}) %collective-permute-start.8) | collective-permute-done | bytes 32800 | tf_op jit(solution)/shard_map/ppermute | solution.py:325
  67.3 0.0 collective-permute-done.9
  67.3 3.0 %collective-permute-done.7 = f32[8,1024]{1,0:T(8,128)S(1)} collective-permute-done((f32[8,1024]{1,0:T(8,128)S(1)}, f32[8,1024]{1,0:T(8,128)S(1)}, u32[]{:S(2)}, u32[]{:S(2)}) %collective-permute-start.7) | collective-permute-done | bytes 32800 | tf_op jit(solution)/shard_map/ppermute | solution.py:325
  70.2 5.4 %collective-permute-start.10 = (f32[8,1024]{1,0:T(8,128)S(1)}, f32[8,1024]{1,0:T(8,128)S(1)}, u32[]{:S(2)}, u32[]{:S(2)}) collective-permute-start(f32[8,1024]{1,0:T(8,128)S(1)} %add_add_fusion), channel_id=1, source_target_pairs={{0,8},{1,9},{2,10},{3,11},{4,12},{5,13},{6,14},{7,15},{8,0},{9,1},... | collective-permute-start | bytes 98312 | tf_op jit(solution)/shard_map/ppermute | solution.py:327
  75.6 3.6 %all-to-all-start.1 = ((bf16[128,8,256]{2,1,0:T(8,128)(2,1)}), bf16[128,8,256]{2,1,0:T(8,128)(2,1)S(1)}, u32[]{:S(2)}, u32[]{:S(2)}) async-start(bf16[128,8,256]{2,1,0:T(8,128)(2,1)} %bitcast.3), calls=%async_computation.1 | async-start | bytes 1048576 | tf_op jit(solution)/shard_map/all_to_all | solution.py:414
  79.2 0.0 collective-permute-done.10
  79.2 0.2 reshape.35
  79.5 0.2 fusion.1
  79.7 0.8 copy.16
  80.6 12.7 %all-to-all-done.1 = bf16[128,8,256]{2,1,0:T(8,128)(2,1)S(1)} async-done(((bf16[128,8,256]{2,1,0:T(8,128)(2,1)}), bf16[128,8,256]{2,1,0:T(8,128)(2,1)S(1)}, u32[]{:S(2)}, u32[]{:S(2)}) %all-to-all-start.1) | async-done | bytes 524320 | tf_op jit(solution)/shard_map/all_to_all | solution.py:414
  93.3 1.1 %shard_map.80 = bf16[16,32,512]{2,1,0:T(8,128)(2,1)} custom-call(bf16[1024,256]{1,0:T(8,128)(2,1)S(1)} %bitcast.20), custom_call_target="tpu_custom_call" | custom-call | tf_op jit(solution)/shard_map/pallas_call | solution.py:425
  (13 shorter events, 0.1 us)
Async XLA Ops:
  0.6 14.3 %copy-start.3 = (f32[16,31,31]{2,0,1:T(8,128)S(1)}, f32[16,31,31]{2,0,1:T(8,128)}, u32[]{:S(2)}) copy-start(f32[16,31,31]{2,0,1:T(8,128)} %param.11) | copy-start | bytes 184516
  3.4 31.1 %all-to-all-start = ((bf16[128,8,512]{2,1,0:T(8,128)(2,1)}), bf16[128,8,512]{2,1,0:T(8,128)(2,1)S(1)}, u32[]{:S(2)}, u32[]{:S(2)}) async-start(bf16[128,8,512]{2,1,0:T(8,128)(2,1)} %bitcast.23), calls=%async_computation | async-start | bytes 2097152 | tf_op jit(solution)/shard_map/all_to_all | solution.py:366
  14.9 2.7 %copy-start = (bf16[512,1536]{1,0:T(8,128)(2,1)S(1)}, bf16[512,1536]{1,0:T(8,128)(2,1)}, u32[]{:S(2)}) copy-start(bf16[512,1536]{1,0:T(8,128)(2,1)} %win_ref.3) | copy-start | bytes 4718596
  14.9 2.7 %copy-start.1 = (bf16[512,512]{1,0:T(8,128)(2,1)S(1)}, bf16[512,512]{1,0:T(8,128)(2,1)}, u32[]{:S(2)}) copy-start(bf16[512,512]{1,0:T(8,128)(2,1)} %wout_ref.1) | copy-start | bytes 1572868
  17.0 17.4 %copy-start.2 = (f32[512]{0:T(512)S(1)}, f32[512]{0:T(512)}, u32[]{:S(2)}) copy-start(f32[512]{0:T(512)} %param.8) | copy-start | bytes 6148
  47.9 1.3 %collective-permute-start = (f32[8,1024]{1,0:T(8,128)S(1)}, f32[8,1024]{1,0:T(8,128)S(1)}, u32[]{:S(2)}, u32[]{:S(2)}) collective-permute-start(f32[8,1024]{1,0:T(8,128)S(1)} %constant_dynamic-slice_fusion), channel_id=1, source_target_pairs={{0,8},{1,9},{2,10},{3,11},{4,12},{5,13},{6,14},{7,15},{8,0},{9,1},... | collective-permute-start | bytes 98312 | tf_op jit(solution)/shard_map/ppermute | solution.py:322
  49.2 4.0 %collective-permute-start.2 = (f32[8,1024]{1,0:T(8,128)S(1)}, f32[8,1024]{1,0:T(8,128)S(1)}, u32[]{:S(2)}, u32[]{:S(2)}) collective-permute-start(f32[8,1024]{1,0:T(8,128)S(1)} %dynamic-slice_add_fusion), channel_id=1, source_target_pairs={{0,32},{8,10},{2,34},{10,12},{4,36},{12,14},{6,38},{14,8},{16,48},... | collective-permute-start | bytes 98312 | tf_op jit(solution)/shard_map/ppermute | solution.py:325
  49.4 3.8 %collective-permute-start.3 = (f32[8,1024]{1,0:T(8,128)S(1)}, f32[8,1024]{1,0:T(8,128)S(1)}, u32[]{:S(2)}, u32[]{:S(2)}) collective-permute-start(f32[8,1024]{1,0:T(8,128)S(1)} %dynamic-slice_add_fusion), channel_id=1, source_target_pairs={{0,96},{8,14},{2,98},{10,8},{4,100},{12,10},{6,102},{14,12},{16,11... | collective-permute-start | bytes 98312 | tf_op jit(solution)/shard_map/ppermute | solution.py:325
  51.9 4.3 %collective-permute-start.1 = (f32[8,1024]{1,0:T(8,128)S(1)}, f32[8,1024]{1,0:T(8,128)S(1)}, u32[]{:S(2)}, u32[]{:S(2)}) collective-permute-start(f32[8,1024]{1,0:T(8,128)S(1)} %dynamic-slice_add_fusion), channel_id=1, source_target_pairs={{0,64},{8,12},{2,66},{10,14},{4,68},{12,8},{6,70},{14,10},{16,80},... | collective-permute-start | bytes 98312 | tf_op jit(solution)/shard_map/ppermute | solution.py:325
  56.2 4.0 %collective-permute-start.5 = (f32[8,1024]{1,0:T(8,128)S(1)}, f32[8,1024]{1,0:T(8,128)S(1)}, u32[]{:S(2)}, u32[]{:S(2)}) collective-permute-start(f32[8,1024]{1,0:T(8,128)S(1)} %add_add_fusion.2), channel_id=1, source_target_pairs={{0,2},{8,24},{2,4},{10,26},{4,6},{12,28},{6,0},{14,30},{16,18},{24... | collective-permute-start | bytes 98312 | tf_op jit(solution)/shard_map/ppermute | solution.py:325
  56.6 3.6 %collective-permute-start.6 = (f32[8,1024]{1,0:T(8,128)S(1)}, f32[8,1024]{1,0:T(8,128)S(1)}, u32[]{:S(2)}, u32[]{:S(2)}) collective-permute-start(f32[8,1024]{1,0:T(8,128)S(1)} %add_add_fusion.2), channel_id=1, source_target_pairs={{0,6},{8,25},{2,0},{10,27},{4,2},{12,29},{6,4},{14,31},{16,22},{24... | collective-permute-start | bytes 98312 | tf_op jit(solution)/shard_map/ppermute | solution.py:325
  58.9 4.3 %collective-permute-start.4 = (f32[8,1024]{1,0:T(8,128)S(1)}, f32[8,1024]{1,0:T(8,128)S(1)}, u32[]{:S(2)}, u32[]{:S(2)}) collective-permute-start(f32[8,1024]{1,0:T(8,128)S(1)} %add_add_fusion.2), channel_id=1, source_target_pairs={{0,4},{8,9},{2,6},{10,11},{4,0},{12,13},{6,2},{14,15},{16,20},{24,... | collective-permute-start | bytes 98312 | tf_op jit(solution)/shard_map/ppermute | solution.py:325
  63.2 4.0 %collective-permute-start.8 = (f32[8,1024]{1,0:T(8,128)S(1)}, f32[8,1024]{1,0:T(8,128)S(1)}, u32[]{:S(2)}, u32[]{:S(2)}) collective-permute-start(f32[8,1024]{1,0:T(8,128)S(1)} %add_add_fusion.1), channel_id=1, source_target_pairs={{0,16},{8,40},{2,18},{10,42},{4,20},{12,44},{6,22},{14,46},{16,1},... | collective-permute-start | bytes 98312 | tf_op jit(solution)/shard_map/ppermute | solution.py:325
  63.8 3.4 %collective-permute-start.9 = (f32[8,1024]{1,0:T(8,128)S(1)}, f32[8,1024]{1,0:T(8,128)S(1)}, u32[]{:S(2)}, u32[]{:S(2)}) collective-permute-start(f32[8,1024]{1,0:T(8,128)S(1)} %add_add_fusion.1), channel_id=1, source_target_pairs={{0,17},{8,104},{2,19},{10,106},{4,21},{12,108},{6,23},{14,110},{16... | collective-permute-start | bytes 98312 | tf_op jit(solution)/shard_map/ppermute | solution.py:325
  66.0 4.3 %collective-permute-start.7 = (f32[8,1024]{1,0:T(8,128)S(1)}, f32[8,1024]{1,0:T(8,128)S(1)}, u32[]{:S(2)}, u32[]{:S(2)}) collective-permute-start(f32[8,1024]{1,0:T(8,128)S(1)} %add_add_fusion.1), channel_id=1, source_target_pairs={{0,1},{8,72},{2,3},{10,74},{4,5},{12,76},{6,7},{14,78},{16,17},{24... | collective-permute-start | bytes 98312 | tf_op jit(solution)/shard_map/ppermute | solution.py:325
  70.2 8.9 %collective-permute-start.10 = (f32[8,1024]{1,0:T(8,128)S(1)}, f32[8,1024]{1,0:T(8,128)S(1)}, u32[]{:S(2)}, u32[]{:S(2)}) collective-permute-start(f32[8,1024]{1,0:T(8,128)S(1)} %add_add_fusion), channel_id=1, source_target_pairs={{0,8},{1,9},{2,10},{3,11},{4,12},{5,13},{6,14},{7,15},{8,0},{9,1},... | collective-permute-start | bytes 98312 | tf_op jit(solution)/shard_map/ppermute | solution.py:327
  75.6 17.6 %all-to-all-start.1 = ((bf16[128,8,256]{2,1,0:T(8,128)(2,1)}), bf16[128,8,256]{2,1,0:T(8,128)(2,1)S(1)}, u32[]{:S(2)}, u32[]{:S(2)}) async-start(bf16[128,8,256]{2,1,0:T(8,128)(2,1)} %bitcast.3), calls=%async_computation.1 | async-start | bytes 1048576 | tf_op jit(solution)/shard_map/all_to_all | solution.py:414
